TPU v7x, 256 devices: a whole 4x4x8 slice. The times are simulated.
256 devices in a mesh: leaf: 8 (over x, core), row: 32 (over y, z).
Axes of the slice: x: 4, y: 4, z: 8, core: 2. Of those that a mesh axis runs over, the one named last changes fastest.
Arguments:
- loc_rhs: float32 [8, 32, 512, 128], P('leaf', 'row'), may hold values from -6 to 6
- loc_inverse: float32 [8, 32, 512, 512], P('leaf', 'row'), may hold values from -0.25 to 0.25
- loc_coupling: float32 [8, 32, 512, 512], P('leaf', 'row'), may hold values from -0.09375 to 0.09375
- loc_pivots: float32 [8, 32, 512], P('leaf', 'row'), may hold values from 0.5 to 4
- pattern: int32 [8, 32, 4], P('leaf', 'row'), may hold values from 0 to 29, as said below
- win_rhs: float32 [4, 2048, 128], P(None, ('leaf', 'row')), may hold values from -6 to 6
- win_pivots: float32 [4, 2048], P(None, ('leaf', 'row')), may hold values from 0.5 to 4
- win_inverse: float32 [32, 120, 2048], P('row', None, 'leaf'), may hold values from -0.125 to 0.125
- win_coupling: float32 [32, 112, 2048], P('row', None, 'leaf'), may hold values from -0.125 to 0.125
Outputs:
- loc_solution: float32 [8, 32, 512, 128], P('leaf', 'row')
- win_solution: float32 [4, 2048, 128], P(None, ('leaf', 'row'))
Inputs may be any that keep to these rules, and one draw needn't show every extreme that they name: `pattern`: on each device the 4 tile numbers are distinct; number p stands for rows p * 128 to (p + 1) * 128 - 1 of the path of the device's leaf index.
All inputs are finite; a program needn't handle non-finite values.
Results may differ from a plain program's by a relative error of at most 0.0001.
Values sent between devices are 32-bit elements; how exact they have to be, the bound alone decides.
A program may use at most 64 MiB of HBM per device.

v0:
```python
import jax
import jax.numpy as jnp
from jax import lax
from jax.sharding import PartitionSpec as P

BASE = 256
TILE = 128


PRECISE = lax.Precision.HIGHEST


def contract_first(left, right):
    return lax.dot_general(left, right, (((0,), (0,)), ((), ())), precision=PRECISE)


def group_sum(partial_value, height, leaf_id, leaf_count):
    group_span = 2**height
    if group_span == 1:
        return partial_value[0]
    padded = jnp.zeros((leaf_count,) + partial_value.shape[1:], jnp.float32)
    padded = lax.dynamic_update_slice_in_dim(
        padded, partial_value, leaf_id // group_span * group_span, 0
    )
    return lax.psum_scatter(padded, "leaf", scatter_dimension=0, tiled=True)[0]


def group_gather(piece, height, leaf_id):
    group_span = 2**height
    if group_span == 1:
        return piece[None]
    whole_set = lax.all_gather(piece[None], "leaf", axis=0, tiled=True)
    return lax.dynamic_slice_in_dim(whole_set, leaf_id // group_span * group_span, group_span, 0)


def masked_block(diag_block, group_span, piece_rows, rank_id, leaf_id):
    row_ids = (
        jnp.arange(group_span)[:, None] * BASE
        + rank_id * piece_rows
        + jnp.arange(piece_rows)[None, :]
    ).reshape(-1)
    col_ids = leaf_id % group_span * BASE + jnp.arange(BASE)
    return jnp.where(col_ids[None, :] < row_ids[:, None], diag_block, 0.0)


def shards(
    loc_rhs,
    loc_inverse,
    loc_coupling,
    loc_pivots,
    pattern,
    win_rhs,
    win_pivots,
    win_inverse,
    win_coupling,
):
    leaf_count = lax.axis_size("leaf")
    rank_count = lax.axis_size("row")
    leaf_id = lax.axis_index("leaf")
    rank_id = lax.axis_index("row")
    levels = win_rhs.shape[0]
    piece_rows = win_rhs.shape[1]
    columns = win_rhs.shape[2]
    groups_total = 2 * leaf_count - 1
    tile_groups = BASE // TILE
    tile_pieces = TILE // piece_rows
    inverse = loc_inverse[0, 0]
    coupling = loc_coupling[0, 0]
    tile_count = coupling.shape[0] // TILE
    own_tiles = pattern[0, 0]
    positions = jnp.arange(inverse.shape[0])
    strict_low = jnp.where(positions[None, :] < positions[:, None], inverse, 0.0)
    solved_loc = loc_rhs[0, 0] + jnp.dot(strict_low, loc_rhs[0, 0], precision=PRECISE)
    loc_terms = jnp.dot(coupling, solved_loc, precision=PRECISE).reshape(
        tile_count, tile_pieces, piece_rows, columns
    )
    slot_ids = jnp.arange(groups_total)[:, None] * tile_groups + jnp.arange(tile_groups)[None, :]
    selector = (slot_ids[:, :, None] == own_tiles[None, None, :]).astype(jnp.float32)
    local_sums = []
    placed = jnp.einsum("ght,tsix->ghsix", selector, loc_terms, precision=PRECISE)
    placed = placed.reshape(groups_total, rank_count, piece_rows, columns)
    padded_levels = []
    for height in range(levels):
        group_span = 2**height
        padded = jnp.zeros((leaf_count, rank_count, piece_rows, columns), jnp.float32)
        segment = placed[group_span - 1 : 2 * group_span - 1]
        padded_levels.append(
            lax.dynamic_update_slice_in_dim(padded, segment, leaf_id // group_span * group_span, 0)
        )
    stacked = jnp.stack(padded_levels).reshape(levels, leaf_count * rank_count, piece_rows, columns)
    summed = lax.psum_scatter(stacked, ("leaf", "row"), scatter_dimension=1, tiled=True)
    for height in range(levels):
        local_sums.append(summed[height, 0])
    from_children = jnp.zeros((piece_rows, columns), jnp.float32)
    solved = []
    diagonals = []
    for height in range(levels):
        group_span = 2**height
        diag_block = win_inverse[
            0, (group_span - 1) * piece_rows : (2 * group_span - 1) * piece_rows
        ]
        strict = masked_block(diag_block, group_span, piece_rows, rank_id, leaf_id)
        diagonals.append(strict)
        residual = win_rhs[height] - local_sums[height] - from_children
        gathered = lax.all_gather(residual, "row", axis=0, tiled=True)
        partial_value = jnp.dot(strict, gathered, precision=PRECISE).reshape(
            group_span, piece_rows, columns
        )
        current = residual + group_sum(partial_value, height, leaf_id, leaf_count)
        solved.append(current)
        if height + 1 < levels:
            spread = lax.all_gather(current, "row", axis=0, tiled=True)
            link_block = win_coupling[
                0, (2 * group_span - 2) * piece_rows : (4 * group_span - 2) * piece_rows
            ]
            coupled = jnp.dot(link_block, spread, precision=PRECISE).reshape(
                2 * group_span, piece_rows, columns
            )
            from_children = group_sum(coupled, height + 1, leaf_id, leaf_count)
    from_parent = jnp.zeros((piece_rows, columns), jnp.float32)
    results = [None] * levels
    spreads = [None] * levels
    for height in reversed(range(levels)):
        group_span = 2**height
        wanted = solved[height] / win_pivots[height][:, None] - from_parent
        rows_in = group_gather(wanted, height, leaf_id)
        partial_value = contract_first(
            diagonals[height], rows_in.reshape(group_span * piece_rows, columns)
        )
        current = wanted + lax.psum_scatter(partial_value, "row", scatter_dimension=0, tiled=True)
        results[height] = current
        spreads[height] = group_gather(current, height, leaf_id)
        if height > 0:
            child_span = group_span // 2
            link_block = win_coupling[
                0, (2 * child_span - 2) * piece_rows : (4 * child_span - 2) * piece_rows
            ]
            partial_value = contract_first(
                link_block, spreads[height].reshape(group_span * piece_rows, columns)
            )
            from_parent = lax.psum_scatter(partial_value, "row", scatter_dimension=0, tiled=True)
    stacked_out = jnp.stack(results)[:, None]
    whole_set = lax.all_gather(stacked_out, ("leaf", "row"), axis=1, tiled=True)
    whole_set = whole_set.reshape(levels, leaf_count, rank_count, piece_rows, columns)
    group_parts = []
    for height in range(levels):
        group_span = 2**height
        group_parts.append(
            lax.dynamic_slice_in_dim(
                whole_set[height], leaf_id // group_span * group_span, group_span, 0
            )
        )
    ordered = jnp.concatenate(group_parts, 0)
    ordered = ordered.reshape(groups_total, tile_groups, tile_pieces, piece_rows, columns)
    picked = jnp.einsum("ght,ghsix->tsix", selector, ordered, precision=PRECISE).reshape(
        tile_count * TILE, columns
    )
    scaled_loc = solved_loc / loc_pivots[0, 0][:, None]
    remainder = scaled_loc - contract_first(coupling, picked)
    answer = remainder + contract_first(strict_low, remainder)
    return (answer[None, None], jnp.stack(results))


def solution(mesh):
    return jax.shard_map(
        shards,
        mesh=mesh,
        in_specs=(
            P("leaf", "row", None, None),
            P("leaf", "row", None, None),
            P("leaf", "row", None, None),
            P("leaf", "row", None),
            P("leaf", "row", None),
            P(None, ("leaf", "row"), None),
            P(None, ("leaf", "row")),
            P("row", None, "leaf"),
            P("row", None, "leaf"),
        ),
        out_specs=(P("leaf", "row", None, None), P(None, ("leaf", "row"), None)),
        check_vma=False,
    )
```

profile of v0, /device:TPU:1, one launch (start us, length us, event | category | flops | bytes accessed | tf_op | source)
XLA Modules:
  0.0 1942.4 jit_solution(597287896424331740)
XLA Ops:
  7.3 2.3 convolution_add_fusion.1
  11.7 2.1 fusion.21
  19.7 2.2 pad_maximum_fusion
  23.4 271.0 %all-reduce.23.cloned.1.call-done = f32[4,256,8,128]{3,2,1,0:T(8,128)} async-done(((f32[4,256,8,128]{3,2,1,0:T(8,128)}), f32[4,256,8,128]{3,2,1,0:T(8,128)}) %all-reduce.23.cloned.1.call-update) | async-done | bytes 4194320
  295.1 34.5 %all_gather.42 = f32[256,128]{1,0:T(8,128)S(1)} all-gather(f32[8,128]{1,0:T(8,128)S(1)} %fusion.107), channel_id=1, replica_groups=mesh['leaf'=8,'row'=32] {'row'}, dimensions={0}, use_global_device_ids=true | all-gather | bytes 135168 | tf_op jit(solution)/shard_map/all_gather | solution.py:105
  329.8 32.6 %all_gather.43 = f32[256,128]{1,0:T(8,128)S(1)} all-gather(f32[8,128]{1,0:T(8,128)S(1)} %convolution_add_fusion.2), channel_id=1, replica_groups=mesh['leaf'=8,'row'=32] {'row'}, dimensions={0}, use_global_device_ids=true | all-gather | bytes 135168 | tf_op jit(solution)/shard_map/all_gather | solution.py:112
  362.5 38.8 %all-reduce.1 = f32[8,8,128]{2,1,0:T(8,128)S(1)} all-reduce(f32[8,8,128]{2,1,0:T(8,128)S(1)} %fusion.14), channel_id=9, replica_groups=mesh['leaf'=8,'row'=32] {'leaf'}, use_global_device_ids=true, to_apply=%region_1.2.clone | all-reduce | flops 8192 | bytes 65536
  402.7 32.9 %all_gather.44 = f32[256,128]{1,0:T(8,128)S(1)} all-gather(f32[8,128]{1,0:T(8,128)S(1)} %fusion.91), channel_id=1, replica_groups=mesh['leaf'=8,'row'=32] {'row'}, dimensions={0}, use_global_device_ids=true | all-gather | bytes 135168 | tf_op jit(solution)/shard_map/all_gather | solution.py:105
  435.8 33.1 %all-reduce.2 = f32[8,8,128]{2,1,0:T(8,128)S(1)} all-reduce(f32[8,8,128]{2,1,0:T(8,128)S(1)} %convolution_dynamic-update-slice_fusion.1), channel_id=10, replica_groups=mesh['leaf'=8,'row'=32] {'leaf'}, use_global_device_ids=true, to_apply=%region_2.3.clone | all-reduce | flops 8192 | bytes 65536
  469.6 30.8 %all_gather.45 = f32[256,128]{1,0:T(8,128)S(1)} all-gather(f32[8,128]{1,0:T(8,128)S(1)} %fusion.93), channel_id=1, replica_groups=mesh['leaf'=8,'row'=32] {'row'}, dimensions={0}, use_global_device_ids=true | all-gather | bytes 135168 | tf_op jit(solution)/shard_map/all_gather | solution.py:112
  500.6 33.7 %all-reduce.3 = f32[8,8,128]{2,1,0:T(8,128)S(1)} all-reduce(f32[8,8,128]{2,1,0:T(8,128)S(1)} %fusion.13), channel_id=11, replica_groups=mesh['leaf'=8,'row'=32] {'leaf'}, use_global_device_ids=true, to_apply=%region_3.4.clone | all-reduce | flops 8192 | bytes 65536
  535.7 32.2 %all_gather.46 = f32[256,128]{1,0:T(8,128)S(1)} all-gather(f32[8,128]{1,0:T(8,128)S(1)} %fusion.95), channel_id=1, replica_groups=mesh['leaf'=8,'row'=32] {'row'}, dimensions={0}, use_global_device_ids=true | all-gather | bytes 135168 | tf_op jit(solution)/shard_map/all_gather | solution.py:105
  568.2 33.7 %all-reduce.4 = f32[8,8,128]{2,1,0:T(8,128)S(1)} all-reduce(f32[8,8,128]{2,1,0:T(8,128)S(1)} %convolution_dynamic-update-slice_fusion), channel_id=12, replica_groups=mesh['leaf'=8,'row'=32] {'leaf'}, use_global_device_ids=true, to_apply=%region_4.5.clone | all-reduce | flops 8192 | bytes 65536
  602.5 30.8 %all_gather.47 = f32[256,128]{1,0:T(8,128)S(1)} all-gather(f32[8,128]{1,0:T(8,128)S(1)} %fusion.97), channel_id=1, replica_groups=mesh['leaf'=8,'row'=32] {'row'}, dimensions={0}, use_global_device_ids=true | all-gather | bytes 135168 | tf_op jit(solution)/shard_map/all_gather | solution.py:112
  633.6 33.7 %all-reduce.5 = f32[8,8,128]{2,1,0:T(8,128)S(1)} all-reduce(f32[8,8,128]{2,1,0:T(8,128)S(1)} %convolution_bitcast_fusion.5), channel_id=13, replica_groups=mesh['leaf'=8,'row'=32] {'leaf'}, use_global_device_ids=true, to_apply=%region_5.6.clone | all-reduce | flops 8192 | bytes 65536
  668.6 32.2 %all_gather.48 = f32[256,128]{1,0:T(8,128)S(1)} all-gather(f32[8,128]{1,0:T(8,128)S(1)} %bitcast_subtract_fusion.1), channel_id=1, replica_groups=mesh['leaf'=8,'row'=32] {'row'}, dimensions={0}, use_global_device_ids=true | all-gather | bytes 135168 | tf_op jit(solution)/shard_map/all_gather | solution.py:105
  701.1 33.7 %all-reduce.6 = f32[8,8,128]{2,1,0:T(8,128)S(1)} all-reduce(f32[8,8,128]{2,1,0:T(8,128)S(1)} %fusion.25), channel_id=14, replica_groups=mesh['leaf'=8,'row'=32] {'leaf'}, use_global_device_ids=true, to_apply=%region_6.7.clone | all-reduce | flops 8192 | bytes 65536
  736.2 16.3 all_gather.49
  755.0 133.2 %all-reduce.25.cloned.1.call-done = f32[256,128]{1,0:T(8,128)} async-done(((f32[256,128]{1,0:T(8,128)}), f32[256,128]{1,0:T(8,128)}) %all-reduce.25.cloned.1.call-update) | async-done | bytes 131088
  889.6 18.0 all-gather
  908.8 135.5 %all-reduce.27.cloned.1.call-done = f32[256,128]{1,0:T(8,128)} async-done(((f32[256,128]{1,0:T(8,128)}), f32[256,128]{1,0:T(8,128)}) %all-reduce.27.cloned.1.call-update) | async-done | bytes 131088
  1045.0 18.0 all-gather.1
  1064.2 135.5 %all-reduce.29.cloned.1.call-done = f32[256,128]{1,0:T(8,128)} async-done(((f32[256,128]{1,0:T(8,128)}), f32[256,128]{1,0:T(8,128)}) %all-reduce.29.cloned.1.call-update) | async-done | bytes 131088
  1200.4 18.0 all-gather.2
  1219.7 135.5 %all-reduce.31.cloned.1.call-done = f32[256,128]{1,0:T(8,128)} async-done(((f32[256,128]{1,0:T(8,128)}), f32[256,128]{1,0:T(8,128)}) %all-reduce.31.cloned.1.call-update) | async-done | bytes 131088
  1355.9 18.0 all-gather.3
  1375.1 135.5 %all-reduce.33.cloned.1.call-done = f32[256,128]{1,0:T(8,128)} async-done(((f32[256,128]{1,0:T(8,128)}), f32[256,128]{1,0:T(8,128)}) %all-reduce.33.cloned.1.call-update) | async-done | bytes 131088
  1511.3 18.0 all-gather.4
  1530.4 135.5 %all-reduce.35.cloned.1.call-done = f32[256,128]{1,0:T(8,128)} async-done(((f32[256,128]{1,0:T(8,128)}), f32[256,128]{1,0:T(8,128)}) %all-reduce.35.cloned.1.call-update) | async-done | bytes 131088
  1667.9 143.1 %all-reduce.37.cloned.1.call-done = f32[256,128]{1,0:T(8,128)} async-done(((f32[256,128]{1,0:T(8,128)}), f32[256,128]{1,0:T(8,128)}) %all-reduce.37.cloned.1.call-update) | async-done | bytes 131088
  1812.3 114.2 %all-gather.8.cloned.1.call-done = f32[4,2048,128]{2,1,0:T(8,128)} async-done(((f32[4,8,128]{2,1,0:T(8,128)}), f32[4,2048,128]{2,1,0:T(8,128)}) %all-gather.8.cloned.1.call-update) | async-done | bytes 4194320 | tf_op jit(solution)/shard_map/all_gather | solution.py:143
  1926.5 2.5 fusion.140
  (117 shorter events, 40.2 us)
Async XLA Ops:
  7.2 2.4 copy-start
  7.2 287.2 %all-reduce.23.cloned.1.call-start = ((), (), s32[]{:S(2)}) async-start(), calls=%async_computation.1 | async-start | bytes 8388608
  16.8 2.7 copy-start.2
  21.9 0.7 copy-start.10
  21.9 1.5 copy-start.6
  21.9 272.5 %copy-start.5 = (f32[4,8,128]{2,1,0:T(8,128)S(1)}, f32[4,8,128]{2,1,0:T(8,128)}, u32[]{:S(2)}) copy-start(f32[4,8,128]{2,1,0:T(8,128)} %param.14) | copy-start | bytes 49156
  22.0 307.6 %copy-start.3 = (f32[1,120,256]{2,1,0:T(8,128)S(1)}, f32[1,120,256]{2,1,0:T(8,128)}, u32[]{:S(2)}) copy-start(f32[1,120,256]{2,1,0:T(8,128)} %param.16) | copy-start | bytes 368644
  22.0 340.4 %copy-start.4 = (f32[1,112,256]{2,1,0:T(8,128)S(1)}, f32[1,112,256]{2,1,0:T(8,128)}, u32[]{:S(2)}) copy-start(f32[1,112,256]{2,1,0:T(8,128)} %param.17) | copy-start | bytes 344068
  22.0 731.9 %copy-start.9 = (u32[256]{0:T(256)S(1)}, u32[256]{0:T(256)}, u32[]{:S(2)}) copy-start(u32[256]{0:T(256)} %constant.167) | copy-start | bytes 3076
  22.0 866.2 %all-reduce.25.cloned.1.call-start = ((), (), s32[]{:S(2)}) async-start(), calls=%async_computation.2 | async-start | bytes 262144
  753.6 290.7 %all-reduce.27.cloned.1.call-start = ((), (), s32[]{:S(2)}) async-start(), calls=%async_computation.3 | async-start | bytes 262144
  908.7 291.1 %all-reduce.29.cloned.1.call-start = ((), (), s32[]{:S(2)}) async-start(), calls=%async_computation.4 | async-start | bytes 262144
  1064.2 291.0 %all-reduce.31.cloned.1.call-start = ((), (), s32[]{:S(2)}) async-start(), calls=%async_computation.5 | async-start | bytes 262144
  1219.5 291.1 %all-reduce.33.cloned.1.call-start = ((), (), s32[]{:S(2)}) async-start(), calls=%async_computation.6 | async-start | bytes 262144
  1375.0 291.0 %all-reduce.35.cloned.1.call-start = ((), (), s32[]{:S(2)}) async-start(), calls=%async_computation.7 | async-start | bytes 262144
  1530.4 280.5 %all-reduce.37.cloned.1.call-start = ((), (), s32[]{:S(2)}) async-start(), calls=%async_computation.8 | async-start | bytes 262144
  1667.8 258.7 %all-gather.8.cloned.1.call-start = ((), (), s32[]{:S(2)}) async-start(), calls=%async_computation | async-start | bytes 4210688 | tf_op jit(solution)/shard_map/all_gather | solution.py:143
  1929.0 1.5 copy-start.8
  1929.1 3.0 copy-start.7
  1930.0 3.9 copy-start.1
Sparse Core Ops, SparseCore 0:
  22.1 272.2 all-reduce.22
  753.7 134.3 all-reduce.24
  908.8 135.4 all-reduce.26
  1064.3 135.4 all-reduce.28
  1219.7 135.4 all-reduce.30
  1375.1 135.4 all-reduce.32
  1530.5 135.4 all-reduce.34
  1670.0 140.8 all-reduce.36
  1815.1 111.3 all-gather.7
where the time goes:
time: 1940 us
  waiting for transfers between devices  1340 us (69%)
  blocking collectives  539 us (28%)
    unnamed x17, waiting for transfers between devices  1220 us
    unnamed x6, blocking collectives  207 us
    all_gather x4, blocking collectives, shards(): gathered = lax.all_gather(residual, 'row', axis=0, tiled=True)  132 us
    all_gather x1, waiting for transfers between devices, shards(): whole_set = lax.all_gather(stacked_out, ('leaf', 'row'), axis=1, tiled=True)  114 us
    all_gather x6, blocking collectives, group_gather(): whole_set = lax.all_gather(piece[None], 'leaf', axis=0, tiled=True)  106 us
    all_gather x3, blocking collectives, shards(): spread = lax.all_gather(current, 'row', axis=0, tiled=True)  94.2 us
  transfers between devices with their start and end apart: 9, of which 9 were waited for; matrix products, arithmetic and copies ran while one was open for 0% of the time, Pallas kernels for 0%

commit v1 on v0

v1 whole, which is shorter than its diff:
```python
import functools

import jax
import jax.numpy as jnp
from jax import lax
from jax.experimental import pallas as pl
from jax.experimental.pallas import tpu as pltpu
from jax.sharding import PartitionSpec as P

MESH = pl.DeviceIdType.MESH
F32 = jnp.float32
BF16 = jnp.bfloat16
NB, NY, NZ, NA, LEVELS = 32, 4, 8, 8, 4


def split(x):
    hi = x.astype(BF16)
    return hi, (x - hi.astype(F32)).astype(BF16)


def mm(left, right, dims=(((1,), (0,)), ((), ()))):
    return lax.dot_general(left, right, dims, preferred_element_type=F32)


def dot3(left, right):
    (lh, ll), (rh, rl) = left, right
    return mm(lh, rh) + (mm(lh, rl) + mm(ll, rh))


def flip(a, d):
    out = a
    for k in range(3):
        if (d >> k) & 1:
            out = out + (1 << k) * (1 - 2 * lax.rem(lax.div(a, 1 << k), 2))
    return out


def at8(value):
    return pl.multiple_of(value, 8)


TOP = [(2**l - 1) * 8 for l in range(LEVELS)]
LINK = [(2 * 2**l - 2) * 8 for l in range(LEVELS)]
SLOT = [0, 0, 1, 4]

PAT, TERM, USUM, PICK = 0, 1, 2, 3
AZ, AY, LU, AG, PX, YX, ZX, XX, RS, PY, BX = 4, 7, 10, 14, 18, 22, 26, 30, 34, 38, 42
NSEM = 46


def kernel(rhs, inv, cpl, piv, pat, wrhs, wpiv, winv, wcpl, out_loc, out_win,
           st_h, st_l, ct_h, ct_l, yloc, zloc, patrecv, sel, tsend, trecv, usend, urecv, ubuf, lurecv,
           strict, aall, bpeer, mbuf, gath, part, precv, yrecv, zbuf, xbuf,
           rsend, rrecv, xpath, psend, precv2, send, recv):
    a = lax.axis_index("leaf")
    b = lax.axis_index("row")
    y = lax.div(b, NZ)
    z = lax.rem(b, NZ)
    own8 = at8(b * 8)

    barrier = pltpu.get_barrier_semaphore()

    def greet(d, carry):
        pl.semaphore_signal(barrier, inc=1, device_id=(a, lax.rem(b + d, NB)), device_id_type=MESH)
        return carry

    lax.fori_loop(1, NB, greet, 0)
    for d in range(1, NA):
        pl.semaphore_signal(barrier, inc=1, device_id=(flip(a, d), b), device_id_type=MESH)

    def push(src, dst, sem, leaf, row):
        pltpu.make_async_remote_copy(
            src_ref=src, dst_ref=dst, send_sem=send.at[sem], recv_sem=recv.at[sem],
            device_id=(leaf, row), device_id_type=MESH,
        ).start()

    def done(which, sem, view):
        pltpu.make_async_copy(view, view, which.at[sem]).wait()

    def zpeers(body):
        def step(d, carry):
            z2 = lax.rem(z + d, NZ)
            body(z2, y * NZ + z2)
            return carry

        lax.fori_loop(1, NZ, step, 0)

    def ypeers(body):
        def step(d, carry):
            body(lax.rem(b + d * NZ, NB))
            return carry

        lax.fori_loop(1, NY, step, 0)

    def rowpeers(body):
        def step(d, carry):
            body(lax.rem(b + d, NB))
            return carry

        lax.fori_loop(1, NB, step, 0)

    for l in range(LEVELS):
        n = 2**l * 8
        rows = lax.broadcasted_iota(jnp.int32, (n, 256), 0)
        cols = lax.broadcasted_iota(jnp.int32, (n, 256), 1)
        row_id = lax.div(rows, 8) * 256 + b * 8 + lax.rem(rows, 8)
        col_id = lax.rem(a, 2**l) * 256 + cols
        block = jnp.where(col_id < row_id, winv[TOP[l] : TOP[l] + n, :], 0.0)
        strict[TOP[l] : TOP[l] + n, :] = block
        if l < 3:
            for q in range(2**l):
                aall[2**l - 1 + q, b] = block[8 * q : 8 * q + 8]
    strict[120:128, :] = jnp.zeros((8, 256), F32)

    lane = lax.broadcasted_iota(jnp.int32, (1, 128), 1)
    for t in range(4):
        tile = pat[0, t]
        mark = lax.rem(tile, 2) * 16 + lax.div(tile, 2)
        patrecv[z, t : t + 1, :] = jnp.where(lane == mark, 1.0, 0.0).astype(F32)

    low_row = lax.broadcasted_iota(jnp.int32, (128, 128), 0)
    low_col = lax.broadcasted_iota(jnp.int32, (128, 128), 1)
    low = low_col < low_row
    right = split(rhs[...])
    for r in range(4):
        acc = rhs[128 * r : 128 * r + 128, :]
        diag = jnp.where(low, inv[128 * r : 128 * r + 128, 128 * r : 128 * r + 128], 0.0)
        acc = acc + dot3(split(diag), (right[0][128 * r : 128 * r + 128], right[1][128 * r : 128 * r + 128]))
        if r:
            acc = acc + dot3(split(inv[128 * r : 128 * r + 128, : 128 * r]), (right[0][: 128 * r], right[1][: 128 * r]))
        yloc[128 * r : 128 * r + 128, :] = acc

    pl.semaphore_wait(barrier, NB - 1 + NA - 1)

    zpeers(lambda z2, row: push(patrecv.at[z], patrecv.at[z], PAT, a, row))
    zpeers(lambda z2, row: push(aall.at[pl.ds(0, 1), b], aall.at[pl.ds(0, 1), b], AZ, a, row))

    solved = split(yloc[...])
    for t in range(4):
        term = dot3(split(cpl[128 * t : 128 * t + 128, :]), solved)
        for i in range(16):
            ih, z2 = divmod(i, 8)
            at = z2 * 64 + t * 16 + ih * 8
            tsend[at : at + 8, :] = term[8 * i : 8 * i + 8]
    own64 = at8(z * 64)
    trecv[pl.ds(own64, 64), :] = tsend[pl.ds(own64, 64), :]
    zpeers(lambda z2, row: push(tsend.at[pl.ds(at8(z2 * 64), 64)], trecv.at[pl.ds(own64, 64)], TERM, a, row))

    for l in (1, 2):
        n = 2**l
        zpeers(lambda z2, row: push(aall.at[pl.ds(n - 1, n), b], aall.at[pl.ds(n - 1, n), b], AZ + l, a, row))
    for d in range(1, 4):
        first = 16 if d == 1 else 48
        push(wcpl.at[pl.ds(first, 112 - first)], bpeer.at[pl.ds(96 * (d - 1) + first - 16, 112 - first)], BX + d, flip(a, d), b)

    def forward_a(l):
        n = 2**l
        done(recv, AZ + l, aall.at[pl.ds(0, n), pl.ds(0, 7)])
        slab = aall.at[pl.ds(n - 1, n), pl.ds(y * NZ, NZ)]
        ypeers(lambda row: push(slab, slab, AY + l, a, row))

    forward_a(0)

    sel[...] = jnp.zeros((128, 128), F32)
    xpath[...] = jnp.zeros((512, 128), F32)
    for r in range(4):
        for c in range(4):
            blk = cpl[128 * r : 128 * r + 128, 128 * c : 128 * c + 128].T
            h, lo = split(blk)
            ct_h[128 * c : 128 * c + 128, 128 * r : 128 * r + 128] = h
            ct_l[128 * c : 128 * c + 128, 128 * r : 128 * r + 128] = lo
            if c <= r:
                blk = inv[128 * r : 128 * r + 128, 128 * c : 128 * c + 128]
                if c == r:
                    blk = jnp.where(low, blk, 0.0)
                h, lo = split(blk.T)
                st_h[128 * c : 128 * c + 128, 128 * r : 128 * r + 128] = h
                st_l[128 * c : 128 * c + 128, 128 * r : 128 * r + 128] = lo
    strict_t = jnp.concatenate([strict[:, :128].T, strict[:, 128:].T], axis=0)
    strict_t = split(strict_t)
    wide = jnp.broadcast_to(piv[...], (128, 512))
    for r in range(4):
        zloc[128 * r : 128 * r + 128, :] = yloc[128 * r : 128 * r + 128, :] / wide[:, 128 * r : 128 * r + 128].T

    done(recv, PAT, patrecv.at[pl.ds(0, 7)])
    for s in range(8):
        sel[4 * s : 4 * s + 4, :] = patrecv[s]
    chosen_t = sel[...].T[:32, :32].astype(BF16)
    done(recv, TERM, trecv.at[pl.ds(0, 448)])
    cols = split(jnp.concatenate([trecv[pl.ds(j, 32, stride=16), :] for j in range(16)], axis=1))
    placed = mm(chosen_t, cols[0]) + mm(chosen_t, cols[1])
    for j in range(16):
        ih, i8 = divmod(j, 8)
        for h in range(2):
            usend[pl.ds(128 * (2 * h + ih) + i8, 16, stride=8), :] = placed[16 * h : 16 * h + 16, 128 * j : 128 * j + 128]
    own128 = at8(y * 128)
    urecv[pl.ds(own128, 128), :] = usend[pl.ds(own128, 128), :]
    ypeers(lambda row: push(usend.at[pl.ds(at8(lax.div(row, NZ) * 128), 128)], urecv.at[pl.ds(own128, 128)], USUM, a, row))

    forward_a(1)
    done(recv, AY, aall.at[pl.ds(0, 1), pl.ds(0, 24)])
    mbuf[0:16, :] = wcpl[0:16, :] + dot3(split(wcpl[0:16, :]), split(aall[0].reshape(256, 256)))
    forward_a(2)

    done(recv, USUM, urecv.at[pl.ds(0, 384)])
    ubuf[...] = (urecv[0:128, :] + urecv[128:256, :]) + (urecv[256:384, :] + urecv[384:512, :])
    for l in range(1, LEVELS):
        for d in range(1, 2**l):
            at = at8(TOP[l] + lax.rem(flip(a, d), 2**l) * 8)
            push(ubuf.at[pl.ds(at, 8)], lurecv.at[pl.ds(8 * (SLOT[l] + d - 1), 8)], LU + l, flip(a, d), b)

    def spread(l, value):
        gath[l, pl.ds(own8, 8), :] = value
        mine = gath.at[l, pl.ds(own8, 8)]
        rowpeers(lambda row: push(mine, mine, AG + l, a, row))

    def load_sum(l):
        total = ubuf[pl.ds(at8(TOP[l] + lax.rem(a, 2**l) * 8), 8), :]
        if l:
            done(recv, LU + l, lurecv.at[pl.ds(0, 8 * (2**l - 1))])
            for d in range(1, 2**l):
                total = total + lurecv[8 * (SLOT[l] + d - 1) : 8 * (SLOT[l] + d), :]
        return total

    eye = lax.broadcasted_iota(jnp.int32, (8, 8), 0) == lax.broadcasted_iota(jnp.int32, (8, 8), 1)

    def pivots(l):
        return jnp.sum(jnp.where(eye, jnp.broadcast_to(wpiv[l : l + 1, :], (8, 8)), 0.0), axis=1, keepdims=True)

    def over_leaves(l, sem, rows, first_slot, slots, count):
        for d in range(1, count):
            at = at8(rows + lax.rem(flip(a, d), count) * 8)
            push(part.at[l, pl.ds(at, 8)], slots.at[pl.ds(8 * (first_slot + d - 1), 8)], sem, flip(a, d), b)

    def collect(sem, slots, first_slot, count, total):
        if count > 1:
            done(recv, sem, slots.at[pl.ds(0, 8 * (count - 1))])
            for d in range(1, count):
                total = total + slots[8 * (first_slot + d - 1) : 8 * (first_slot + d), :]
        return total

    def form_m(l):
        n = 2**l
        rows = 2 * n * 8
        done(recv, AY + l, aall.at[pl.ds(0, n), pl.ds(0, 24)])
        own = wcpl[LINK[l] : LINK[l] + rows, :]
        total = own
        for d in range(n):
            if d == 0:
                left = own
            else:
                if l == 2 or d == 1:
                    if not (l == 2 and d == 1):
                        first = 16 if d == 1 else 48
                        done(recv, BX + d, wcpl.at[pl.ds(first, 112 - first)])
                at = 96 * (d - 1) + LINK[l] - 16
                left = bpeer[at : at + rows, :]
            block = aall[n - 1 + lax.rem(flip(a, d), n)].reshape(256, 256)
            total = total + dot3(split(left), split(block))
        mbuf[LINK[l] : LINK[l] + rows, :] = total

    def keep_z(l, res, own_part):
        value = collect(YX + l, yrecv, SLOT[l], 2**l, res + own_part)
        value = value / pivots(l)
        at = at8(TOP[l] + lax.rem(a, 2**l) * 8)
        zbuf[pl.ds(at, 8), :] = value
        mine = zbuf.at[pl.ds(at, 8)]
        for d in range(1, 2**l):
            push(mine, mine, ZX + l, flip(a, d), b)
        return value

    below = None
    zs = []
    pending = None
    for l in range(LEVELS):
        n = 2**l
        res = wrhs[l] - load_sum(l)
        if l:
            res = res - below
        spread(l, res)
        if l in (1, 2):
            form_m(l)
        if pending is not None:
            zs.append(keep_z(l - 1, *pending))
        lhs = strict[TOP[l] : TOP[l] + 8 * n, :]
        if l < 3:
            lhs = jnp.concatenate([lhs, mbuf[LINK[l] : LINK[l] + 16 * n, :]], axis=0)
        lhs = split(lhs)
        done(recv, AG + l, gath.at[l, pl.ds(0, 248)])
        out = dot3(lhs, split(gath[l]))
        part[l, pl.ds(0, out.shape[0]), :] = out
        if l < 3:
            over_leaves(l, PX + l, 8 * n, SLOT[l + 1], precv, 2 * n)
        over_leaves(l, YX + l, 0, SLOT[l], yrecv, n)
        own_y = part[l, pl.ds(at8(lax.rem(a, n) * 8), 8), :]
        if l < 3:
            below = part[l, pl.ds(at8(8 * n + lax.rem(a, 2 * n) * 8), 8), :]
            below = collect(PX + l, precv, SLOT[l + 1], 2 * n, below)
        pending = (res, own_y)
    zs.append(keep_z(3, *pending))

    def fill(value, first):
        before = [jnp.zeros((first, 128), F32)] if first else []
        after = 128 - first - value.shape[0]
        return split(jnp.concatenate(before + [value] + ([jnp.zeros((after, 128), F32)] if after else []), axis=0))

    def own_half(l):
        n = 2**l
        if l:
            done(recv, ZX + l, zbuf.at[pl.ds(0, 8 * (n - 1))])
        return dot3(strict_t, fill(zbuf[TOP[l] : TOP[l] + 8 * n, :], TOP[l]))

    def reduce_rows(l, value, total):
        rsend[l] = value
        rrecv[l, pl.ds(own8, 8), :] = rsend[l, pl.ds(own8, 8), :]
        rowpeers(lambda row: push(rsend.at[l, pl.ds(at8(row * 8), 8)], rrecv.at[l, pl.ds(own8, 8)], RS + l, a, row))

    def reduced(l, total):
        done(recv, RS + l, rrecv.at[l, pl.ds(0, 248)])
        sums = [rrecv[l, 8 * s : 8 * s + 8, :] for s in range(NB)]
        while len(sums) > 1:
            sums = [sums[2 * k] + sums[2 * k + 1] for k in range(len(sums) // 2)]
        return total + sums[0]

    reduce_rows(3, own_half(3), None)
    m_t = jnp.concatenate([mbuf[0:112, :], jnp.zeros((16, 256), F32)], axis=0)
    m_t = split(jnp.concatenate([m_t[:, :128].T, m_t[:, 128:].T], axis=0))
    for l in reversed(range(LEVELS)):
        n = 2**l
        if l:
            ahead = own_half(l - 1)
        value = reduced(l, zs[l])
        out_win[l] = value
        at = at8(TOP[l] + lax.rem(a, n) * 8)
        xbuf[pl.ds(at, 8), :] = value
        mine = xbuf.at[pl.ds(at, 8)]
        for d in range(1, n):
            push(mine, mine, XX + l, flip(a, d), b)
        if l:
            done(recv, XX + l, xbuf.at[pl.ds(0, 8 * (n - 1))])
            level = xbuf[TOP[l] : TOP[l] + 8 * n, :]
            reduce_rows(l - 1, ahead - dot3(m_t, fill(level, LINK[l - 1])), None)
        block = xbuf.at[pl.ds(TOP[l], 8 * n)]
        there = xpath.at[pl.ds(at8(y * 128 + TOP[l]), 8 * n)]
        ypeers(lambda row: push(block, there, PY + l, a, row))
        xpath[pl.ds(at8(y * 128 + TOP[l]), 8 * n), :] = xbuf[TOP[l] : TOP[l] + 8 * n, :]

    for l in range(LEVELS):
        done(recv, PY + l, xpath.at[pl.ds(0, 24 * 2**l)])
    chosen = sel[0:32, 0:32].astype(BF16)
    pieces = []
    for j in range(16):
        ih, i8 = divmod(j, 8)
        pieces.append(jnp.concatenate([xpath[pl.ds(128 * (2 * h + ih) + i8, 16, stride=8), :] for h in range(2)], axis=0))
    pieces = split(jnp.concatenate(pieces, axis=1))
    picked = mm(chosen, pieces[0]) + mm(chosen, pieces[1])
    for j in range(16):
        psend[pl.ds(j, 32, stride=16), :] = picked[:, 128 * j : 128 * j + 128]
    precv2[pl.ds(own64, 64), :] = psend[pl.ds(own64, 64), :]
    zpeers(lambda z2, row: push(psend.at[pl.ds(at8(z2 * 64), 64)], precv2.at[pl.ds(own64, 64)], PICK, a, row))
    done(recv, PICK, precv2.at[pl.ds(0, 448)])
    rows = []
    for t in range(4):
        for i in range(16):
            ih, z2 = divmod(i, 8)
            at = z2 * 64 + t * 16 + ih * 8
            rows.append(precv2[at : at + 8, :])
    got = split(jnp.concatenate(rows, axis=0))
    for r in range(4):
        s = slice(128 * r, 128 * r + 128)
        yloc[s, :] = zloc[s, :] - dot3((ct_h[s, :], ct_l[s, :]), got)
    after = split(yloc[...])
    for r in range(4):
        s = slice(128 * r, 128 * r + 128)
        k = slice(128 * r, 512)
        out_loc[s, :] = yloc[s, :] + dot3((st_h[s, k], st_l[s, k]), (after[0][k], after[1][k]))

    done(send, PAT, patrecv.at[pl.ds(0, 7)])
    done(send, TERM, trecv.at[pl.ds(0, 448)])
    done(send, USUM, urecv.at[pl.ds(0, 384)])
    done(send, PICK, precv2.at[pl.ds(0, 448)])
    for l in range(LEVELS):
        n = 2**l
        if l < 3:
            done(send, AZ + l, aall.at[pl.ds(0, n), pl.ds(0, 7)])
            done(send, AY + l, aall.at[pl.ds(0, n), pl.ds(0, 24)])
            done(send, PX + l, precv.at[pl.ds(0, 8 * (2 * n - 1))])
        if l:
            done(send, LU + l, lurecv.at[pl.ds(0, 8 * (n - 1))])
            done(send, YX + l, yrecv.at[pl.ds(0, 8 * (n - 1))])
            done(send, ZX + l, zbuf.at[pl.ds(0, 8 * (n - 1))])
            done(send, XX + l, xbuf.at[pl.ds(0, 8 * (n - 1))])
        done(send, AG + l, gath.at[l, pl.ds(0, 248)])
        done(send, RS + l, rrecv.at[l, pl.ds(0, 248)])
        done(send, PY + l, xpath.at[pl.ds(0, 24 * n)])
    for d in range(1, 4):
        first = 16 if d == 1 else 48
        done(send, BX + d, wcpl.at[pl.ds(first, 112 - first)])


def shards(loc_rhs, loc_inverse, loc_coupling, loc_pivots, pattern, win_rhs, win_pivots, win_inverse, win_coupling):
    vmem = pl.BlockSpec(memory_space=pltpu.VMEM)
    specs = [vmem] * 9
    specs[4] = pl.BlockSpec(memory_space=pltpu.SMEM)
    out_loc, out_win = pl.pallas_call(
        kernel,
        out_shape=(jax.ShapeDtypeStruct((512, 128), F32), jax.ShapeDtypeStruct((LEVELS, 8, 128), F32)),
        in_specs=specs,
        out_specs=(vmem, vmem),
        scratch_shapes=[
            pltpu.VMEM((512, 512), BF16),
            pltpu.VMEM((512, 512), BF16),
            pltpu.VMEM((512, 512), BF16),
            pltpu.VMEM((512, 512), BF16),
            pltpu.VMEM((512, 128), F32),
            pltpu.VMEM((512, 128), F32),
            pltpu.VMEM((8, 4, 128), F32),
            pltpu.VMEM((128, 128), F32),
            pltpu.VMEM((512, 128), F32),
            pltpu.VMEM((512, 128), F32),
            pltpu.VMEM((512, 128), F32),
            pltpu.VMEM((512, 128), F32),
            pltpu.VMEM((128, 128), F32),
            pltpu.VMEM((88, 128), F32),
            pltpu.VMEM((128, 256), F32),
            pltpu.VMEM((7, NB, 8, 256), F32),
            pltpu.VMEM((288, 256), F32),
            pltpu.VMEM((112, 256), F32),
            pltpu.VMEM((LEVELS, 256, 128), F32),
            pltpu.VMEM((LEVELS, 96, 128), F32),
            pltpu.VMEM((88, 128), F32),
            pltpu.VMEM((88, 128), F32),
            pltpu.VMEM((120, 128), F32),
            pltpu.VMEM((120, 128), F32),
            pltpu.VMEM((LEVELS, 256, 128), F32),
            pltpu.VMEM((LEVELS, 256, 128), F32),
            pltpu.VMEM((512, 128), F32),
            pltpu.VMEM((512, 128), F32),
            pltpu.VMEM((512, 128), F32),
            pltpu.SemaphoreType.DMA((NSEM,)),
            pltpu.SemaphoreType.DMA((NSEM,)),
        ],
        compiler_params=pltpu.CompilerParams(collective_id=0, has_side_effects=True, vmem_limit_bytes=40 << 20),
    )(
        loc_rhs[0, 0], loc_inverse[0, 0], loc_coupling[0, 0], loc_pivots[0], pattern[0],
        win_rhs, win_pivots, win_inverse[0], win_coupling[0],
    )
    return out_loc[None, None], out_win


def solution(mesh):
    return jax.shard_map(
        shards,
        mesh=mesh,
        in_specs=(
            P("leaf", "row", None, None),
            P("leaf", "row", None, None),
            P("leaf", "row", None, None),
            P("leaf", "row", None),
            P("leaf", "row", None),
            P(None, ("leaf", "row"), None),
            P(None, ("leaf", "row")),
            P("row", None, "leaf"),
            P("row", None, "leaf"),
        ),
        out_specs=(P("leaf", "row", None, None), P(None, ("leaf", "row"), None)),
        check_vma=False,
    )
```

time: 1940 us -> 141 us (0.07)
  waiting for transfers between devices: 1340 us -> 0 us
  blocking collectives: 539 us -> 0 us
  Pallas kernels: 0 us -> 132 us
    unnamed x17 -> x0, waiting for transfers between devices: 1220 us -> none
    all_gather x13 -> x0, blocking collectives: 332 us -> none  [the longest x4 132 us: shards(): gathered = lax.all_gather(residual, 'row', axis=0, tiled=True)]
    unnamed x6 -> x0, blocking collectives: 207 us -> none
    pallas_call x0 -> x1, Pallas kernels: none -> 132 us  [shards(): pl.pallas_call(kernel, out_shape=(jax.ShapeDtypeStruct((512, 128), F32),...]
    all_gather x1 -> x0, waiting for transfers between devices: 114 us -> none  [shards(): whole_set = lax.all_gather(stacked_out, ('leaf', 'row'), axis=1, tiled=True)]
  transfers between devices with their start and end apart: 9 -> 0, of which waited for: 9 -> 0; matrix products, arithmetic and copies ran while one was open for 0% -> 0% of each run, Pallas kernels for 0% -> 0%
where the time goes in v1:
time: 141 us
  Pallas kernels  132 us (94%)
  local copies, waits for them, and re-layouts  7.9 us (6%)
    pallas_call x1, Pallas kernels, shards(): pl.pallas_call(kernel, out_shape=(jax.ShapeDtypeStruct((512, 128), F32),...  132 us
    unnamed x20, local copies, waits for them, and re-layouts  7.9 us

profile of v1, /device:TPU:1, one launch (start us, length us, event | category | flops | bytes accessed | tf_op | source)
XLA Modules:
  0.0 140.5 jit_solution(3740745223778265181)
XLA Ops:
  0.6 0.0 copy-start.7
  0.6 0.0 copy-start.6
  0.7 0.0 copy-start.8
  0.7 0.7 copy-done.7
  1.3 0.0 copy-done.6
  1.3 0.0 copy-done.8
  1.3 0.0 copy-start
  1.3 1.2 copy-done
  2.6 0.0 copy-start.1
  2.6 1.2 copy-done.1
  3.8 0.0 copy-start.2
  3.8 0.9 copy-done.2
  4.7 0.0 copy-start.3
  4.7 0.9 copy-done.3
  5.6 0.0 copy-start.4
  5.6 0.9 copy-done.4
  6.5 0.0 copy-start.5
  6.5 0.7 copy-done.5
  7.3 132.0 %shard_map.104 = (f32[512,128]{1,0:T(8,128)S(1)}, f32[4,8,128]{2,1,0:T(8,128)S(1)}) custom-call(f32[512,128]{1,0:T(8,128)S(1)} %bitcast.11, f32[512,512]{1,0:T(8,128)S(1)} %bitcast.8, f32[512,512]{1,0:T(8,128)S(1)} %bitcast.9, f32[1,512]{1,0:T(1,128)S(1)} %bitcast.14, s32[1,4]{1,0:T(1,128)S(1)} %bitcast.15, f32[4,8,128]{2,1,0:T(8,128)S(1)} %copy-done.5, ...), custom_call_target="tpu_custom_call" | custom-call | tf_op jit(solution)/shard_map/pallas_call | solution.py:405
  139.2 0.7 copy.13
  139.9 0.6 copy.14
Async XLA Ops:
  0.6 0.7 copy-start.7
  0.6 0.7 copy-start.6
  0.7 0.7 copy-start.8
  1.3 1.2 copy-start
  2.6 1.2 copy-start.1
  3.8 0.9 copy-start.2
  4.7 0.9 copy-start.3
  5.6 0.9 copy-start.4
  6.5 0.7 copy-start.5

commit v2 on v1

--- a/solution.py
+++ b/solution.py
@@ -45,10 +45,12 @@
 
 PAT, TERM, USUM, PICK = 0, 1, 2, 3
 AZ, AY, LU, AG, PX, YX, ZX, XX, RS, PY, BX = 4, 7, 10, 14, 18, 22, 26, 30, 34, 38, 42
-NSEM = 46
-
-
-def kernel(rhs, inv, cpl, piv, pat, wrhs, wpiv, winv, wcpl, out_loc, out_win,
+U0, X0 = 46, 47
+NSEM = 48
+
+
+def kernel(rhs_in, inv_in, cpl_in, piv_in, pat_in, wrhs_in, wpiv_in, winv_in, wcpl_in, out_loc, out_win,
+           rhs, inv, cpl, piv, pat, wrhs, wpiv, winv, wcpl, u0send, u0recv, x0all, loads,
            st_h, st_l, ct_h, ct_l, yloc, zloc, patrecv, sel, tsend, trecv, usend, urecv, ubuf, lurecv,
            strict, aall, bpeer, mbuf, gath, part, precv, yrecv, zbuf, xbuf,
            rsend, rrecv, xpath, psend, precv2, send, recv):
@@ -58,6 +60,12 @@
     z = lax.rem(b, NZ)
     own8 = at8(b * 8)
 
+    pairs = [(pat_in, pat), (rhs_in, rhs), (inv_in, inv), (winv_in, winv), (cpl_in, cpl),
+             (wcpl_in, wcpl), (piv_in, piv), (wrhs_in, wrhs), (wpiv_in, wpiv)]
+    fetch = [pltpu.make_async_copy(src, dst, loads.at[k]) for k, (src, dst) in enumerate(pairs)]
+    for copy in fetch:
+        copy.start()
+
     barrier = pltpu.get_barrier_semaphore()
 
     def greet(d, carry):
@@ -99,6 +107,10 @@
 
         lax.fori_loop(1, NB, step, 0)
 
+    sel[...] = jnp.zeros((128, 128), F32)
+    xpath[...] = jnp.zeros((512, 128), F32)
+
+    fetch[3].wait()
     for l in range(LEVELS):
         n = 2**l * 8
         rows = lax.broadcasted_iota(jnp.int32, (n, 256), 0)
@@ -112,15 +124,20 @@
                 aall[2**l - 1 + q, b] = block[8 * q : 8 * q + 8]
     strict[120:128, :] = jnp.zeros((8, 256), F32)
 
+    fetch[0].wait()
     lane = lax.broadcasted_iota(jnp.int32, (1, 128), 1)
+    base = []
     for t in range(4):
         tile = pat[0, t]
+        base.append([jnp.where(jnp.full((1, 128), tile, jnp.int32) == p, 1.0, 0.0).astype(F32) for p in range(2)])
         mark = lax.rem(tile, 2) * 16 + lax.div(tile, 2)
         patrecv[z, t : t + 1, :] = jnp.where(lane == mark, 1.0, 0.0).astype(F32)
 
     low_row = lax.broadcasted_iota(jnp.int32, (128, 128), 0)
     low_col = lax.broadcasted_iota(jnp.int32, (128, 128), 1)
     low = low_col < low_row
+    fetch[1].wait()
+    fetch[2].wait()
     right = split(rhs[...])
     for r in range(4):
         acc = rhs[128 * r : 128 * r + 128, :]
@@ -136,15 +153,24 @@
     zpeers(lambda z2, row: push(aall.at[pl.ds(0, 1), b], aall.at[pl.ds(0, 1), b], AZ, a, row))
 
     solved = split(yloc[...])
+    fetch[4].wait()
+    low0, low1 = 0.0, 0.0
     for t in range(4):
         term = dot3(split(cpl[128 * t : 128 * t + 128, :]), solved)
+        low0 = low0 + base[t][0] * term
+        low1 = low1 + base[t][1] * term
         for i in range(16):
             ih, z2 = divmod(i, 8)
             at = z2 * 64 + t * 16 + ih * 8
             tsend[at : at + 8, :] = term[8 * i : 8 * i + 8]
+    u0send[0:128, :] = low0
+    u0send[128:256, :] = low1
+    rowpeers(lambda row: push(u0send.at[pl.ds(at8(row * 8), 8)], u0recv.at[pl.ds(own8, 8)], U0, a, row))
+    u0recv[pl.ds(own8, 8), :] = u0send[pl.ds(own8, 8), :]
     own64 = at8(z * 64)
+    zpeers(lambda z2, row: push(tsend.at[pl.ds(at8(z2 * 64), 64)], trecv.at[pl.ds(own64, 64)], TERM, a, row))
     trecv[pl.ds(own64, 64), :] = tsend[pl.ds(own64, 64), :]
-    zpeers(lambda z2, row: push(tsend.at[pl.ds(at8(z2 * 64), 64)], trecv.at[pl.ds(own64, 64)], TERM, a, row))
+    fetch[5].wait()
 
     for l in (1, 2):
         n = 2**l
@@ -161,8 +187,6 @@
 
     forward_a(0)
 
-    sel[...] = jnp.zeros((128, 128), F32)
-    xpath[...] = jnp.zeros((512, 128), F32)
     for r in range(4):
         for c in range(4):
             blk = cpl[128 * r : 128 * r + 128, 128 * c : 128 * c + 128].T
@@ -178,36 +202,44 @@
                 st_l[128 * c : 128 * c + 128, 128 * r : 128 * r + 128] = lo
     strict_t = jnp.concatenate([strict[:, :128].T, strict[:, 128:].T], axis=0)
     strict_t = split(strict_t)
+    fetch[6].wait()
     wide = jnp.broadcast_to(piv[...], (128, 512))
     for r in range(4):
         zloc[128 * r : 128 * r + 128, :] = yloc[128 * r : 128 * r + 128, :] / wide[:, 128 * r : 128 * r + 128].T
 
-    done(recv, PAT, patrecv.at[pl.ds(0, 7)])
-    for s in range(8):
-        sel[4 * s : 4 * s + 4, :] = patrecv[s]
-    chosen_t = sel[...].T[:32, :32].astype(BF16)
-    done(recv, TERM, trecv.at[pl.ds(0, 448)])
-    cols = split(jnp.concatenate([trecv[pl.ds(j, 32, stride=16), :] for j in range(16)], axis=1))
-    placed = mm(chosen_t, cols[0]) + mm(chosen_t, cols[1])
-    for j in range(16):
-        ih, i8 = divmod(j, 8)
-        for h in range(2):
-            usend[pl.ds(128 * (2 * h + ih) + i8, 16, stride=8), :] = placed[16 * h : 16 * h + 16, 128 * j : 128 * j + 128]
-    own128 = at8(y * 128)
-    urecv[pl.ds(own128, 128), :] = usend[pl.ds(own128, 128), :]
-    ypeers(lambda row: push(usend.at[pl.ds(at8(lax.div(row, NZ) * 128), 128)], urecv.at[pl.ds(own128, 128)], USUM, a, row))
-
-    forward_a(1)
-    done(recv, AY, aall.at[pl.ds(0, 1), pl.ds(0, 24)])
-    mbuf[0:16, :] = wcpl[0:16, :] + dot3(split(wcpl[0:16, :]), split(aall[0].reshape(256, 256)))
-    forward_a(2)
-
-    done(recv, USUM, urecv.at[pl.ds(0, 384)])
-    ubuf[...] = (urecv[0:128, :] + urecv[128:256, :]) + (urecv[256:384, :] + urecv[384:512, :])
-    for l in range(1, LEVELS):
-        for d in range(1, 2**l):
-            at = at8(TOP[l] + lax.rem(flip(a, d), 2**l) * 8)
-            push(ubuf.at[pl.ds(at, 8)], lurecv.at[pl.ds(8 * (SLOT[l] + d - 1), 8)], LU + l, flip(a, d), b)
+    def tree(ref):
+        sums = [ref[8 * s : 8 * s + 8, :] for s in range(NB)]
+        while len(sums) > 1:
+            sums = [sums[2 * k] + sums[2 * k + 1] for k in range(len(sums) // 2)]
+        return sums[0]
+
+    def place_terms():
+        done(recv, PAT, patrecv.at[pl.ds(0, 7)])
+        for s in range(8):
+            sel[4 * s : 4 * s + 4, :] = patrecv[s]
+        chosen_t = sel[...].T[:32, :32].astype(BF16)
+        done(recv, TERM, trecv.at[pl.ds(0, 448)])
+        cols = split(jnp.concatenate([trecv[pl.ds(j, 32, stride=16), :] for j in range(16)], axis=1))
+        placed = mm(chosen_t, cols[0]) + mm(chosen_t, cols[1])
+        for j in range(16):
+            ih, i8 = divmod(j, 8)
+            for h in range(2):
+                usend[pl.ds(128 * (2 * h + ih) + i8, 16, stride=8), :] = placed[16 * h : 16 * h + 16, 128 * j : 128 * j + 128]
+        own128 = at8(y * 128)
+        ypeers(lambda row: push(usend.at[pl.ds(at8(lax.div(row, NZ) * 128 + 8), 112)], urecv.at[pl.ds(at8(own128 + 8), 112)], USUM, a, row))
+        urecv[pl.ds(own128, 128), :] = usend[pl.ds(own128, 128), :]
+
+    def sum_terms():
+        done(recv, USUM, urecv.at[pl.ds(0, 336)])
+        ubuf[8:120, :] = (urecv[8:120, :] + urecv[136:248, :]) + (urecv[264:376, :] + urecv[392:504, :])
+        for l in range(1, LEVELS):
+            for d in range(1, 2**l):
+                at = at8(TOP[l] + lax.rem(flip(a, d), 2**l) * 8)
+                push(ubuf.at[pl.ds(at, 8)], lurecv.at[pl.ds(8 * (SLOT[l] + d - 1), 8)], LU + l, flip(a, d), b)
+
+    def form_m0():
+        done(recv, AY, aall.at[pl.ds(0, 1), pl.ds(0, 24)])
+        mbuf[0:16, :] = wcpl[0:16, :] + dot3(split(wcpl[0:16, :]), split(aall[0].reshape(256, 256)))
 
     def spread(l, value):
         gath[l, pl.ds(own8, 8), :] = value
@@ -216,10 +248,9 @@
 
     def load_sum(l):
         total = ubuf[pl.ds(at8(TOP[l] + lax.rem(a, 2**l) * 8), 8), :]
-        if l:
-            done(recv, LU + l, lurecv.at[pl.ds(0, 8 * (2**l - 1))])
-            for d in range(1, 2**l):
-                total = total + lurecv[8 * (SLOT[l] + d - 1) : 8 * (SLOT[l] + d), :]
+        done(recv, LU + l, lurecv.at[pl.ds(0, 8 * (2**l - 1))])
+        for d in range(1, 2**l):
+            total = total + lurecv[8 * (SLOT[l] + d - 1) : 8 * (SLOT[l] + d), :]
         return total
 
     eye = lax.broadcasted_iota(jnp.int32, (8, 8), 0) == lax.broadcasted_iota(jnp.int32, (8, 8), 1)
@@ -272,12 +303,21 @@
     below = None
     zs = []
     pending = None
+    fetch[7].wait()
+    fetch[8].wait()
     for l in range(LEVELS):
         n = 2**l
-        res = wrhs[l] - load_sum(l)
         if l:
-            res = res - below
+            res = wrhs[l] - load_sum(l) - below
+        else:
+            done(recv, U0, u0recv.at[pl.ds(0, 248)])
+            res = wrhs[0] - tree(u0recv)
         spread(l, res)
+        if l == 0:
+            place_terms()
+            forward_a(1)
+            form_m0()
+            forward_a(2)
         if l in (1, 2):
             form_m(l)
         if pending is not None:
@@ -293,6 +333,8 @@
             over_leaves(l, PX + l, 8 * n, SLOT[l + 1], precv, 2 * n)
         over_leaves(l, YX + l, 0, SLOT[l], yrecv, n)
         own_y = part[l, pl.ds(at8(lax.rem(a, n) * 8), 8), :]
+        if l == 0:
+            sum_terms()
         if l < 3:
             below = part[l, pl.ds(at8(8 * n + lax.rem(a, 2 * n) * 8), 8), :]
             below = collect(PX + l, precv, SLOT[l + 1], 2 * n, below)
@@ -317,10 +359,7 @@
 
     def reduced(l, total):
         done(recv, RS + l, rrecv.at[l, pl.ds(0, 248)])
-        sums = [rrecv[l, 8 * s : 8 * s + 8, :] for s in range(NB)]
-        while len(sums) > 1:
-            sums = [sums[2 * k] + sums[2 * k + 1] for k in range(len(sums) // 2)]
-        return total + sums[0]
+        return total + tree(rrecv.at[l])
 
     reduce_rows(3, own_half(3), None)
     m_t = jnp.concatenate([mbuf[0:112, :], jnp.zeros((16, 256), F32)], axis=0)
@@ -329,42 +368,50 @@
         n = 2**l
         if l:
             ahead = own_half(l - 1)
+        else:
+            for m in range(1, LEVELS):
+                done(recv, PY + m, xpath.at[pl.ds(0, 24 * 2**m)])
+            chosen = sel[0:32, 0:32].astype(BF16)
+            pieces = []
+            for j in range(16):
+                ih, i8 = divmod(j, 8)
+                pieces.append(jnp.concatenate([xpath[pl.ds(128 * (2 * h + ih) + i8, 16, stride=8), :] for h in range(2)], axis=0))
+            pieces = split(jnp.concatenate(pieces, axis=1))
+            picked = mm(chosen, pieces[0]) + mm(chosen, pieces[1])
+            for j in range(16):
+                psend[pl.ds(j, 32, stride=16), :] = picked[:, 128 * j : 128 * j + 128]
+            zpeers(lambda z2, row: push(psend.at[pl.ds(at8(z2 * 64), 64)], precv2.at[pl.ds(own64, 64)], PICK, a, row))
+            precv2[pl.ds(own64, 64), :] = psend[pl.ds(own64, 64), :]
         value = reduced(l, zs[l])
-        out_win[l] = value
-        at = at8(TOP[l] + lax.rem(a, n) * 8)
-        xbuf[pl.ds(at, 8), :] = value
-        mine = xbuf.at[pl.ds(at, 8)]
-        for d in range(1, n):
-            push(mine, mine, XX + l, flip(a, d), b)
         if l:
+            at = at8(TOP[l] + lax.rem(a, n) * 8)
+            xbuf[pl.ds(at, 8), :] = value
+            mine = xbuf.at[pl.ds(at, 8)]
+            for d in range(1, n):
+                push(mine, mine, XX + l, flip(a, d), b)
+            out_win[l] = value
             done(recv, XX + l, xbuf.at[pl.ds(0, 8 * (n - 1))])
             level = xbuf[TOP[l] : TOP[l] + 8 * n, :]
             reduce_rows(l - 1, ahead - dot3(m_t, fill(level, LINK[l - 1])), None)
-        block = xbuf.at[pl.ds(TOP[l], 8 * n)]
-        there = xpath.at[pl.ds(at8(y * 128 + TOP[l]), 8 * n)]
-        ypeers(lambda row: push(block, there, PY + l, a, row))
-        xpath[pl.ds(at8(y * 128 + TOP[l]), 8 * n), :] = xbuf[TOP[l] : TOP[l] + 8 * n, :]
-
-    for l in range(LEVELS):
-        done(recv, PY + l, xpath.at[pl.ds(0, 24 * 2**l)])
-    chosen = sel[0:32, 0:32].astype(BF16)
-    pieces = []
-    for j in range(16):
-        ih, i8 = divmod(j, 8)
-        pieces.append(jnp.concatenate([xpath[pl.ds(128 * (2 * h + ih) + i8, 16, stride=8), :] for h in range(2)], axis=0))
-    pieces = split(jnp.concatenate(pieces, axis=1))
-    picked = mm(chosen, pieces[0]) + mm(chosen, pieces[1])
-    for j in range(16):
-        psend[pl.ds(j, 32, stride=16), :] = picked[:, 128 * j : 128 * j + 128]
-    precv2[pl.ds(own64, 64), :] = psend[pl.ds(own64, 64), :]
-    zpeers(lambda z2, row: push(psend.at[pl.ds(at8(z2 * 64), 64)], precv2.at[pl.ds(own64, 64)], PICK, a, row))
+            block = xbuf.at[pl.ds(TOP[l], 8 * n)]
+            there = xpath.at[pl.ds(at8(y * 128 + TOP[l]), 8 * n)]
+            ypeers(lambda row: push(block, there, PY + l, a, row))
+            xpath[pl.ds(at8(y * 128 + TOP[l]), 8 * n), :] = level
+        else:
+            x0all[pl.ds(own8, 8), :] = value
+            mine = x0all.at[pl.ds(own8, 8)]
+            rowpeers(lambda row: push(mine, mine, X0, a, row))
+            out_win[0] = value
+
     done(recv, PICK, precv2.at[pl.ds(0, 448)])
+    done(recv, X0, x0all.at[pl.ds(0, 248)])
     rows = []
     for t in range(4):
         for i in range(16):
             ih, z2 = divmod(i, 8)
             at = z2 * 64 + t * 16 + ih * 8
-            rows.append(precv2[at : at + 8, :])
+            here = base[t][0] * x0all[8 * i : 8 * i + 8, :] + base[t][1] * x0all[128 + 8 * i : 136 + 8 * i, :]
+            rows.append(precv2[at : at + 8, :] + here)
     got = split(jnp.concatenate(rows, axis=0))
     for r in range(4):
         s = slice(128 * r, 128 * r + 128)
@@ -377,7 +424,9 @@
 
     done(send, PAT, patrecv.at[pl.ds(0, 7)])
     done(send, TERM, trecv.at[pl.ds(0, 448)])
-    done(send, USUM, urecv.at[pl.ds(0, 384)])
+    done(send, USUM, urecv.at[pl.ds(0, 336)])
+    done(send, U0, u0recv.at[pl.ds(0, 248)])
+    done(send, X0, x0all.at[pl.ds(0, 248)])
     done(send, PICK, precv2.at[pl.ds(0, 448)])
     for l in range(LEVELS):
         n = 2**l
@@ -392,7 +441,8 @@
             done(send, XX + l, xbuf.at[pl.ds(0, 8 * (n - 1))])
         done(send, AG + l, gath.at[l, pl.ds(0, 248)])
         done(send, RS + l, rrecv.at[l, pl.ds(0, 248)])
-        done(send, PY + l, xpath.at[pl.ds(0, 24 * n)])
+        if l:
+            done(send, PY + l, xpath.at[pl.ds(0, 24 * n)])
     for d in range(1, 4):
         first = 16 if d == 1 else 48
         done(send, BX + d, wcpl.at[pl.ds(first, 112 - first)])
@@ -400,14 +450,26 @@
 
 def shards(loc_rhs, loc_inverse, loc_coupling, loc_pivots, pattern, win_rhs, win_pivots, win_inverse, win_coupling):
     vmem = pl.BlockSpec(memory_space=pltpu.VMEM)
-    specs = [vmem] * 9
-    specs[4] = pl.BlockSpec(memory_space=pltpu.SMEM)
+    specs = [pl.BlockSpec(memory_space=pl.ANY)] * 9
     out_loc, out_win = pl.pallas_call(
         kernel,
         out_shape=(jax.ShapeDtypeStruct((512, 128), F32), jax.ShapeDtypeStruct((LEVELS, 8, 128), F32)),
         in_specs=specs,
         out_specs=(vmem, vmem),
         scratch_shapes=[
+            pltpu.VMEM((512, 128), F32),
+            pltpu.VMEM((512, 512), F32),
+            pltpu.VMEM((512, 512), F32),
+            pltpu.VMEM((1, 512), F32),
+            pltpu.SMEM((1, 4), jnp.int32),
+            pltpu.VMEM((LEVELS, 8, 128), F32),
+            pltpu.VMEM((LEVELS, 8), F32),
+            pltpu.VMEM((120, 256), F32),
+            pltpu.VMEM((112, 256), F32),
+            pltpu.VMEM((256, 128), F32),
+            pltpu.VMEM((256, 128), F32),
+            pltpu.VMEM((256, 128), F32),
+            pltpu.SemaphoreType.DMA((9,)),
             pltpu.VMEM((512, 512), BF16),
             pltpu.VMEM((512, 512), BF16),
             pltpu.VMEM((512, 512), BF16),
@@ -440,7 +502,7 @@
             pltpu.SemaphoreType.DMA((NSEM,)),
             pltpu.SemaphoreType.DMA((NSEM,)),
         ],
-        compiler_params=pltpu.CompilerParams(collective_id=0, has_side_effects=True, vmem_limit_bytes=40 << 20),
+        compiler_params=pltpu.CompilerParams(collective_id=0, has_side_effects=True),
     )(
         loc_rhs[0, 0], loc_inverse[0, 0], loc_coupling[0, 0], loc_pivots[0], pattern[0],
         win_rhs, win_pivots, win_inverse[0], win_coupling[0],

time: 141 us -> 129 us (0.915)
  Pallas kernels: 132 us -> 126 us
  local copies, waits for them, and re-layouts: 7.9 us -> 2.28 us
    pallas_call x1, Pallas kernels: 132 us -> 126 us  [shards(): pl.pallas_call(kernel, out_shape=(jax.ShapeDtypeStruct((512, 128), F32),...]
    unnamed x20 -> x4, local copies, waits for them, and re-layouts: 7.9 us -> 2.28 us
where the time goes in v2:
time: 129 us
  Pallas kernels  126 us (98%)
  local copies, waits for them, and re-layouts  2.28 us (2%)
    pallas_call x1, Pallas kernels, shards(): pl.pallas_call(kernel, out_shape=(jax.ShapeDtypeStruct((512, 128), F32),...  126 us

profile of v2, /device:TPU:1, one launch (start us, length us, event | category | flops | bytes accessed | tf_op | source)
XLA Modules:
  0.0 129.0 jit_solution(4079775463526074421)
XLA Ops:
  0.6 126.0 %shard_map.104 = (f32[512,128]{1,0:T(8,128)}, f32[4,8,128]{2,1,0:T(8,128)}) custom-call(f32[512,128]{1,0:T(8,128)} %bitcast.11, f32[512,512]{1,0:T(8,128)} %bitcast.8, f32[512,512]{1,0:T(8,128)} %bitcast.9, f32[1,512]{1,0:T(1,128)} %bitcast.14, s32[1,4]{1,0:T(1,128)} %bitcast.15, f32[4,8,128]{2,1,0:T(8,128)} %wrhs_in.1, f32[4,8]{1,0:T(4,128)} %wpiv_in.1, ...), custom_call_target="tpu_custom_call" | custom-call | tf_op jit(solution)/shard_map/pallas_call | solution.py:454
  126.7 0.0 copy-start
  126.7 1.7 %copy.13 = f32[1,1,512,128]{3,2,1,0:T(8,128)} copy(f32[1,1,512,128]{3,2,1,0:T(8,128)} %bitcast.10) | data formatting | bytes 524288
  128.3 0.0 copy-done
  128.3 0.6 copy.14
Async XLA Ops:
  126.7 1.7 %copy-start = (f32[4,8,128]{2,1,0:T(8,128)S(1)}, f32[4,8,128]{2,1,0:T(8,128)}, u32[]{:S(2)}) copy-start(f32[4,8,128]{2,1,0:T(8,128)} %get-tuple-element.9) | copy-start | bytes 49156

commit v3 on v2

--- a/solution.py
+++ b/solution.py
@@ -24,7 +24,11 @@
 
 def dot3(left, right):
     (lh, ll), (rh, rl) = left, right
-    return mm(lh, rh) + (mm(lh, rl) + mm(ll, rh))
+    n = rh.shape[1]
+    if n != 128:
+        return mm(lh, rh) + (mm(lh, rl) + mm(ll, rh))
+    both = mm(lh, jnp.concatenate([rh, rl], axis=1))
+    return both[:, :n] + (both[:, n:] + mm(ll, rh))
 
 
 def flip(a, d):
@@ -45,12 +49,12 @@
 
 PAT, TERM, USUM, PICK = 0, 1, 2, 3
 AZ, AY, LU, AG, PX, YX, ZX, XX, RS, PY, BX = 4, 7, 10, 14, 18, 22, 26, 30, 34, 38, 42
-U0, X0 = 46, 47
-NSEM = 48
+U0, X1, MZ, MY, ZA = 46, 47, 48, 49, 50
+NSEM = 51
 
 
 def kernel(rhs_in, inv_in, cpl_in, piv_in, pat_in, wrhs_in, wpiv_in, winv_in, wcpl_in, out_loc, out_win,
-           rhs, inv, cpl, piv, pat, wrhs, wpiv, winv, wcpl, u0send, u0recv, x0all, loads,
+           rhs, inv, cpl, piv, pat, wrhs, wpiv, winv, wcpl, u0send, u0recv, x0all, x1all, z0all, c0, m0all, m0t_h, m0t_l, loads,
            st_h, st_l, ct_h, ct_l, yloc, zloc, patrecv, sel, tsend, trecv, usend, urecv, ubuf, lurecv,
            strict, aall, bpeer, mbuf, gath, part, precv, yrecv, zbuf, xbuf,
            rsend, rrecv, xpath, psend, precv2, send, recv):
@@ -82,30 +86,58 @@
             device_id=(leaf, row), device_id_type=MESH,
         ).start()
 
-    def done(which, sem, view):
-        pltpu.make_async_copy(view, view, which.at[sem]).wait()
+    views = {PAT: patrecv.at[pl.ds(0, 7)], TERM: trecv.at[pl.ds(0, 448)], USUM: urecv.at[pl.ds(0, 336)],
+             PICK: precv2.at[pl.ds(0, 448)], U0: u0recv.at[pl.ds(0, 248)],
+             X1: x1all.at[:, pl.ds(0, 31)], MZ: m0all.at[:, pl.ds(0, 7)], MY: m0all.at[:, pl.ds(0, 24)],
+             ZA: z0all.at[pl.ds(0, 248)]}
+    for l in range(LEVELS):
+        n = 2**l
+        views[AG + l] = gath.at[l, pl.ds(0, 248)]
+        if l < 3:
+            views[AZ + l] = aall.at[pl.ds(0, n), pl.ds(0, 7)]
+            views[AY + l] = aall.at[pl.ds(0, n), pl.ds(0, 24)]
+            views[PX + l] = precv.at[pl.ds(0, 8 * (2 * n - 1))]
+        if l:
+            views[RS + l] = rrecv.at[l, pl.ds(0, 248)]
+            views[LU + l] = lurecv.at[pl.ds(0, 8 * (n - 1))]
+            views[YX + l] = yrecv.at[pl.ds(0, 8 * (n - 1))]
+            views[ZX + l] = zbuf.at[pl.ds(0, 8 * (n - 1))]
+            views[XX + l] = xbuf.at[pl.ds(0, 8 * (n - 1))]
+        if l > 1:
+            views[PY + l] = xpath.at[pl.ds(0, 24 * n)]
+    for d in range(1, 4):
+        first = 16 if d == 1 else 48
+        views[BX + d] = wcpl.at[pl.ds(first, 112 - first)]
+
+    def done(which, sem):
+        pltpu.make_async_copy(views[sem], views[sem], which.at[sem]).wait()
+
+    def around(k, n):
+        return n // 2 + lax.div(k + 1, 2) * (1 - 2 * lax.rem(k, 2))
 
     def zpeers(body):
-        def step(d, carry):
-            z2 = lax.rem(z + d, NZ)
+        def step(k, carry):
+            z2 = lax.rem(z + around(k, NZ), NZ)
             body(z2, y * NZ + z2)
             return carry
 
-        lax.fori_loop(1, NZ, step, 0)
+        lax.fori_loop(0, NZ - 1, step, 0)
 
     def ypeers(body):
-        def step(d, carry):
-            body(lax.rem(b + d * NZ, NB))
+        def step(k, carry):
+            body(lax.rem(y + around(k, NY), NY) * NZ + z)
             return carry
 
-        lax.fori_loop(1, NY, step, 0)
+        lax.fori_loop(0, NY - 1, step, 0)
 
     def rowpeers(body):
-        def step(d, carry):
-            body(lax.rem(b + d, NB))
+        def step(k, carry):
+            y2 = lax.rem(y + around(lax.rem(k, NY), NY), NY)
+            z2 = lax.rem(z + around(lax.div(k, NY), NZ), NZ)
+            body(y2 * NZ + z2)
             return carry
 
-        lax.fori_loop(1, NB, step, 0)
+        lax.fori_loop(0, NB - 1, step, 0)
 
     sel[...] = jnp.zeros((128, 128), F32)
     xpath[...] = jnp.zeros((512, 128), F32)
@@ -129,7 +161,7 @@
     base = []
     for t in range(4):
         tile = pat[0, t]
-        base.append([jnp.where(jnp.full((1, 128), tile, jnp.int32) == p, 1.0, 0.0).astype(F32) for p in range(2)])
+        base.append([jnp.where(jnp.full((1, 128), tile, jnp.int32) == p, 1.0, 0.0).astype(F32) for p in range(6)])
         mark = lax.rem(tile, 2) * 16 + lax.div(tile, 2)
         patrecv[z, t : t + 1, :] = jnp.where(lane == mark, 1.0, 0.0).astype(F32)
 
@@ -150,7 +182,9 @@
     pl.semaphore_wait(barrier, NB - 1 + NA - 1)
 
     zpeers(lambda z2, row: push(patrecv.at[z], patrecv.at[z], PAT, a, row))
-    zpeers(lambda z2, row: push(aall.at[pl.ds(0, 1), b], aall.at[pl.ds(0, 1), b], AZ, a, row))
+    for l in range(3):
+        n = 2**l
+        zpeers(lambda z2, row: push(aall.at[pl.ds(n - 1, n), b], aall.at[pl.ds(n - 1, n), b], AZ + l, a, row))
 
     solved = split(yloc[...])
     fetch[4].wait()
@@ -172,20 +206,18 @@
     trecv[pl.ds(own64, 64), :] = tsend[pl.ds(own64, 64), :]
     fetch[5].wait()
 
-    for l in (1, 2):
-        n = 2**l
-        zpeers(lambda z2, row: push(aall.at[pl.ds(n - 1, n), b], aall.at[pl.ds(n - 1, n), b], AZ + l, a, row))
     for d in range(1, 4):
         first = 16 if d == 1 else 48
         push(wcpl.at[pl.ds(first, 112 - first)], bpeer.at[pl.ds(96 * (d - 1) + first - 16, 112 - first)], BX + d, flip(a, d), b)
 
-    def forward_a(l):
-        n = 2**l
-        done(recv, AZ + l, aall.at[pl.ds(0, n), pl.ds(0, 7)])
-        slab = aall.at[pl.ds(n - 1, n), pl.ds(y * NZ, NZ)]
+    def forward_a(l, first, count):
+        slab = aall.at[pl.ds(2**l - 1 + first, count), pl.ds(y * NZ, NZ)]
         ypeers(lambda row: push(slab, slab, AY + l, a, row))
 
-    forward_a(0)
+    done(recv, AZ)
+    forward_a(0, 0, 1)
+    done(recv, AZ + 1)
+    forward_a(1, 0, 2)
 
     for r in range(4):
         for c in range(4):
@@ -214,11 +246,11 @@
         return sums[0]
 
     def place_terms():
-        done(recv, PAT, patrecv.at[pl.ds(0, 7)])
+        done(recv, PAT)
         for s in range(8):
             sel[4 * s : 4 * s + 4, :] = patrecv[s]
         chosen_t = sel[...].T[:32, :32].astype(BF16)
-        done(recv, TERM, trecv.at[pl.ds(0, 448)])
+        done(recv, TERM)
         cols = split(jnp.concatenate([trecv[pl.ds(j, 32, stride=16), :] for j in range(16)], axis=1))
         placed = mm(chosen_t, cols[0]) + mm(chosen_t, cols[1])
         for j in range(16):
@@ -230,7 +262,7 @@
         urecv[pl.ds(own128, 128), :] = usend[pl.ds(own128, 128), :]
 
     def sum_terms():
-        done(recv, USUM, urecv.at[pl.ds(0, 336)])
+        done(recv, USUM)
         ubuf[8:120, :] = (urecv[8:120, :] + urecv[136:248, :]) + (urecv[264:376, :] + urecv[392:504, :])
         for l in range(1, LEVELS):
             for d in range(1, 2**l):
@@ -238,7 +270,7 @@
                 push(ubuf.at[pl.ds(at, 8)], lurecv.at[pl.ds(8 * (SLOT[l] + d - 1), 8)], LU + l, flip(a, d), b)
 
     def form_m0():
-        done(recv, AY, aall.at[pl.ds(0, 1), pl.ds(0, 24)])
+        done(recv, AY)
         mbuf[0:16, :] = wcpl[0:16, :] + dot3(split(wcpl[0:16, :]), split(aall[0].reshape(256, 256)))
 
     def spread(l, value):
@@ -248,7 +280,7 @@
 
     def load_sum(l):
         total = ubuf[pl.ds(at8(TOP[l] + lax.rem(a, 2**l) * 8), 8), :]
-        done(recv, LU + l, lurecv.at[pl.ds(0, 8 * (2**l - 1))])
+        done(recv, LU + l)
         for d in range(1, 2**l):
             total = total + lurecv[8 * (SLOT[l] + d - 1) : 8 * (SLOT[l] + d), :]
         return total
@@ -265,7 +297,7 @@
 
     def collect(sem, slots, first_slot, count, total):
         if count > 1:
-            done(recv, sem, slots.at[pl.ds(0, 8 * (count - 1))])
+            done(recv, sem)
             for d in range(1, count):
                 total = total + slots[8 * (first_slot + d - 1) : 8 * (first_slot + d), :]
         return total
@@ -273,7 +305,7 @@
     def form_m(l):
         n = 2**l
         rows = 2 * n * 8
-        done(recv, AY + l, aall.at[pl.ds(0, n), pl.ds(0, 24)])
+        done(recv, AY + l)
         own = wcpl[LINK[l] : LINK[l] + rows, :]
         total = own
         for d in range(n):
@@ -283,7 +315,7 @@
                 if l == 2 or d == 1:
                     if not (l == 2 and d == 1):
                         first = 16 if d == 1 else 48
-                        done(recv, BX + d, wcpl.at[pl.ds(first, 112 - first)])
+                        done(recv, BX + d)
                 at = 96 * (d - 1) + LINK[l] - 16
                 left = bpeer[at : at + rows, :]
             block = aall[n - 1 + lax.rem(flip(a, d), n)].reshape(256, 256)
@@ -310,14 +342,24 @@
         if l:
             res = wrhs[l] - load_sum(l) - below
         else:
-            done(recv, U0, u0recv.at[pl.ds(0, 248)])
+            done(recv, U0)
             res = wrhs[0] - tree(u0recv)
         spread(l, res)
         if l == 0:
             place_terms()
-            forward_a(1)
+            done(recv, AZ + 2)
+            forward_a(2, 0, 2)
             form_m0()
-            forward_a(2)
+            for q in range(2):
+                m0all[q, b] = mbuf[8 * q : 8 * q + 8, :]
+        if l == 1:
+            forward_a(2, 2, 2)
+        if l == 2:
+            zpeers(lambda z2, row: push(m0all.at[:, b], m0all.at[:, b], MZ, a, row))
+        if l == 3:
+            done(recv, MZ)
+            slab0 = m0all.at[:, pl.ds(y * NZ, NZ)]
+            ypeers(lambda row: push(slab0, slab0, MY, a, row))
         if l in (1, 2):
             form_m(l)
         if pending is not None:
@@ -326,7 +368,7 @@
         if l < 3:
             lhs = jnp.concatenate([lhs, mbuf[LINK[l] : LINK[l] + 16 * n, :]], axis=0)
         lhs = split(lhs)
-        done(recv, AG + l, gath.at[l, pl.ds(0, 248)])
+        done(recv, AG + l)
         out = dot3(lhs, split(gath[l]))
         part[l, pl.ds(0, out.shape[0]), :] = out
         if l < 3:
@@ -340,6 +382,8 @@
             below = collect(PX + l, precv, SLOT[l + 1], 2 * n, below)
         pending = (res, own_y)
     zs.append(keep_z(3, *pending))
+    z0all[pl.ds(own8, 8), :] = zs[0]
+    rowpeers(lambda row: push(z0all.at[pl.ds(own8, 8)], z0all.at[pl.ds(own8, 8)], ZA, a, row))
 
     def fill(value, first):
         before = [jnp.zeros((first, 128), F32)] if first else []
@@ -349,7 +393,7 @@
     def own_half(l):
         n = 2**l
         if l:
-            done(recv, ZX + l, zbuf.at[pl.ds(0, 8 * (n - 1))])
+            done(recv, ZX + l)
         return dot3(strict_t, fill(zbuf[TOP[l] : TOP[l] + 8 * n, :], TOP[l]))
 
     def reduce_rows(l, value, total):
@@ -358,19 +402,32 @@
         rowpeers(lambda row: push(rsend.at[l, pl.ds(at8(row * 8), 8)], rrecv.at[l, pl.ds(own8, 8)], RS + l, a, row))
 
     def reduced(l, total):
-        done(recv, RS + l, rrecv.at[l, pl.ds(0, 248)])
+        done(recv, RS + l)
         return total + tree(rrecv.at[l])
 
     reduce_rows(3, own_half(3), None)
     m_t = jnp.concatenate([mbuf[0:112, :], jnp.zeros((16, 256), F32)], axis=0)
     m_t = split(jnp.concatenate([m_t[:, :128].T, m_t[:, 128:].T], axis=0))
-    for l in reversed(range(LEVELS)):
+    done(recv, MY)
+    for q in range(4):
+        for c in range(2):
+            blk = m0all[q // 2, 16 * (q % 2) : 16 * (q % 2) + 16].reshape(128, 256)[:, 128 * c : 128 * c + 128]
+            h, lo = split(blk.T)
+            m0t_h[128 * c : 128 * c + 128, 128 * q : 128 * q + 128] = h
+            m0t_l[128 * c : 128 * c + 128, 128 * q : 128 * q + 128] = lo
+
+    for l in (3, 2, 1):
         n = 2**l
-        if l:
+        if l > 1:
             ahead = own_half(l - 1)
-        else:
-            for m in range(1, LEVELS):
-                done(recv, PY + m, xpath.at[pl.ds(0, 24 * 2**m)])
+        if l == 2:
+            done(recv, ZA)
+            a0 = aall[0].reshape(256, 256)
+            a0 = jnp.concatenate([a0[:, :128].T, a0[:, 128:].T], axis=0)
+            c0[...] = z0all[...] + dot3(split(a0), split(z0all[...]))
+        if l == 1:
+            for m in (2, 3):
+                done(recv, PY + m)
             chosen = sel[0:32, 0:32].astype(BF16)
             pieces = []
             for j in range(16):
@@ -383,35 +440,40 @@
             zpeers(lambda z2, row: push(psend.at[pl.ds(at8(z2 * 64), 64)], precv2.at[pl.ds(own64, 64)], PICK, a, row))
             precv2[pl.ds(own64, 64), :] = psend[pl.ds(own64, 64), :]
         value = reduced(l, zs[l])
-        if l:
-            at = at8(TOP[l] + lax.rem(a, n) * 8)
-            xbuf[pl.ds(at, 8), :] = value
-            mine = xbuf.at[pl.ds(at, 8)]
-            for d in range(1, n):
-                push(mine, mine, XX + l, flip(a, d), b)
-            out_win[l] = value
-            done(recv, XX + l, xbuf.at[pl.ds(0, 8 * (n - 1))])
-            level = xbuf[TOP[l] : TOP[l] + 8 * n, :]
+        at = at8(TOP[l] + lax.rem(a, n) * 8)
+        xbuf[pl.ds(at, 8), :] = value
+        mine = xbuf.at[pl.ds(at, 8)]
+        for d in range(1, n):
+            push(mine, mine, XX + l, flip(a, d), b)
+        out_win[l] = value
+        done(recv, XX + l)
+        level = xbuf[TOP[l] : TOP[l] + 8 * n, :]
+        if l > 1:
             reduce_rows(l - 1, ahead - dot3(m_t, fill(level, LINK[l - 1])), None)
             block = xbuf.at[pl.ds(TOP[l], 8 * n)]
             there = xpath.at[pl.ds(at8(y * 128 + TOP[l]), 8 * n)]
             ypeers(lambda row: push(block, there, PY + l, a, row))
             xpath[pl.ds(at8(y * 128 + TOP[l]), 8 * n), :] = level
         else:
-            x0all[pl.ds(own8, 8), :] = value
-            mine = x0all.at[pl.ds(own8, 8)]
-            rowpeers(lambda row: push(mine, mine, X0, a, row))
-            out_win[0] = value
-
-    done(recv, PICK, precv2.at[pl.ds(0, 448)])
-    done(recv, X0, x0all.at[pl.ds(0, 248)])
+            for q in range(2):
+                x1all[q, b] = level[8 * q : 8 * q + 8]
+            rowpeers(lambda row: push(x1all.at[:, b], x1all.at[:, b], X1, a, row))
+
+    done(recv, X1)
+    x1 = x1all[...].reshape(512, 128)
+    x0all[...] = c0[...] - dot3((m0t_h[...], m0t_l[...]), split(x1))
+    out_win[0] = x0all[pl.ds(own8, 8), :]
+    tiles = [x0all[0:128, :], x0all[128:256, :]] + [x1[128 * q : 128 * q + 128] for q in range(4)]
+    done(recv, PICK)
     rows = []
     for t in range(4):
         for i in range(16):
             ih, z2 = divmod(i, 8)
             at = z2 * 64 + t * 16 + ih * 8
-            here = base[t][0] * x0all[8 * i : 8 * i + 8, :] + base[t][1] * x0all[128 + 8 * i : 136 + 8 * i, :]
-            rows.append(precv2[at : at + 8, :] + here)
+            here = precv2[at : at + 8, :]
+            for p in range(6):
+                here = here + base[t][p] * tiles[p][8 * i : 8 * i + 8]
+            rows.append(here)
     got = split(jnp.concatenate(rows, axis=0))
     for r in range(4):
         s = slice(128 * r, 128 * r + 128)
@@ -422,30 +484,8 @@
         k = slice(128 * r, 512)
         out_loc[s, :] = yloc[s, :] + dot3((st_h[s, k], st_l[s, k]), (after[0][k], after[1][k]))
 
-    done(send, PAT, patrecv.at[pl.ds(0, 7)])
-    done(send, TERM, trecv.at[pl.ds(0, 448)])
-    done(send, USUM, urecv.at[pl.ds(0, 336)])
-    done(send, U0, u0recv.at[pl.ds(0, 248)])
-    done(send, X0, x0all.at[pl.ds(0, 248)])
-    done(send, PICK, precv2.at[pl.ds(0, 448)])
-    for l in range(LEVELS):
-        n = 2**l
-        if l < 3:
-            done(send, AZ + l, aall.at[pl.ds(0, n), pl.ds(0, 7)])
-            done(send, AY + l, aall.at[pl.ds(0, n), pl.ds(0, 24)])
-            done(send, PX + l, precv.at[pl.ds(0, 8 * (2 * n - 1))])
-        if l:
-            done(send, LU + l, lurecv.at[pl.ds(0, 8 * (n - 1))])
-            done(send, YX + l, yrecv.at[pl.ds(0, 8 * (n - 1))])
-            done(send, ZX + l, zbuf.at[pl.ds(0, 8 * (n - 1))])
-            done(send, XX + l, xbuf.at[pl.ds(0, 8 * (n - 1))])
-        done(send, AG + l, gath.at[l, pl.ds(0, 248)])
-        done(send, RS + l, rrecv.at[l, pl.ds(0, 248)])
-        if l:
-            done(send, PY + l, xpath.at[pl.ds(0, 24 * n)])
-    for d in range(1, 4):
-        first = 16 if d == 1 else 48
-        done(send, BX + d, wcpl.at[pl.ds(first, 112 - first)])
+    for sem in views:
+        done(send, sem)
 
 
 def shards(loc_rhs, loc_inverse, loc_coupling, loc_pivots, pattern, win_rhs, win_pivots, win_inverse, win_coupling):
@@ -469,6 +509,12 @@
             pltpu.VMEM((256, 128), F32),
             pltpu.VMEM((256, 128), F32),
             pltpu.VMEM((256, 128), F32),
+            pltpu.VMEM((2, NB, 8, 128), F32),
+            pltpu.VMEM((256, 128), F32),
+            pltpu.VMEM((256, 128), F32),
+            pltpu.VMEM((2, NB, 8, 256), F32),
+            pltpu.VMEM((256, 512), BF16),
+            pltpu.VMEM((256, 512), BF16),
             pltpu.SemaphoreType.DMA((9,)),
             pltpu.VMEM((512, 512), BF16),
             pltpu.VMEM((512, 512), BF16),

time: 129 us -> 118 us (0.915)
  Pallas kernels: 126 us -> 115 us
    pallas_call x1, Pallas kernels: 126 us -> 115 us  [shards(): pl.pallas_call(kernel, out_shape=(jax.ShapeDtypeStruct((512, 128), F32),...]
where the time goes in v3:
time: 118 us
  Pallas kernels  115 us (97%)
  local copies, waits for them, and re-layouts  2.28 us (2%)
    pallas_call x1, Pallas kernels, shards(): pl.pallas_call(kernel, out_shape=(jax.ShapeDtypeStruct((512, 128), F32),...  115 us

profile of v3, /device:TPU:1, one launch (start us, length us, event | category | flops | bytes accessed | tf_op | source)
XLA Modules:
  0.0 117.6 jit_solution(5279090777538086115)
XLA Ops:
  0.6 114.7 %shard_map.104 = (f32[512,128]{1,0:T(8,128)}, f32[4,8,128]{2,1,0:T(8,128)}) custom-call(f32[512,128]{1,0:T(8,128)} %bitcast.11, f32[512,512]{1,0:T(8,128)} %bitcast.8, f32[512,512]{1,0:T(8,128)} %bitcast.9, f32[1,512]{1,0:T(1,128)} %bitcast.14, s32[1,4]{1,0:T(1,128)} %bitcast.15, f32[4,8,128]{2,1,0:T(8,128)} %wrhs_in.1, f32[4,8]{1,0:T(4,128)} %wpiv_in.1, ...), custom_call_target="tpu_custom_call" | custom-call | tf_op jit(solution)/shard_map/pallas_call | solution.py:494
  115.4 0.0 copy-start
  115.4 1.7 %copy.13 = f32[1,1,512,128]{3,2,1,0:T(8,128)} copy(f32[1,1,512,128]{3,2,1,0:T(8,128)} %bitcast.10) | data formatting | bytes 524288
  117.0 0.0 copy-done
  117.0 0.6 copy.14
Async XLA Ops:
  115.4 1.7 %copy-start = (f32[4,8,128]{2,1,0:T(8,128)S(1)}, f32[4,8,128]{2,1,0:T(8,128)}, u32[]{:S(2)}) copy-start(f32[4,8,128]{2,1,0:T(8,128)} %get-tuple-element.9) | copy-start | bytes 49156

commit v4 on v3

--- a/solution.py
+++ b/solution.py
@@ -165,6 +165,13 @@
         mark = lax.rem(tile, 2) * 16 + lax.div(tile, 2)
         patrecv[z, t : t + 1, :] = jnp.where(lane == mark, 1.0, 0.0).astype(F32)
 
+    pl.semaphore_wait(barrier, NB - 1 + NA - 1)
+
+    zpeers(lambda z2, row: push(patrecv.at[z], patrecv.at[z], PAT, a, row))
+    for l in range(2):
+        n = 2**l
+        zpeers(lambda z2, row: push(aall.at[pl.ds(n - 1, n), b], aall.at[pl.ds(n - 1, n), b], AZ + l, a, row))
+
     low_row = lax.broadcasted_iota(jnp.int32, (128, 128), 0)
     low_col = lax.broadcasted_iota(jnp.int32, (128, 128), 1)
     low = low_col < low_row
@@ -178,13 +185,6 @@
         if r:
             acc = acc + dot3(split(inv[128 * r : 128 * r + 128, : 128 * r]), (right[0][: 128 * r], right[1][: 128 * r]))
         yloc[128 * r : 128 * r + 128, :] = acc
-
-    pl.semaphore_wait(barrier, NB - 1 + NA - 1)
-
-    zpeers(lambda z2, row: push(patrecv.at[z], patrecv.at[z], PAT, a, row))
-    for l in range(3):
-        n = 2**l
-        zpeers(lambda z2, row: push(aall.at[pl.ds(n - 1, n), b], aall.at[pl.ds(n - 1, n), b], AZ + l, a, row))
 
     solved = split(yloc[...])
     fetch[4].wait()
@@ -346,14 +346,14 @@
             res = wrhs[0] - tree(u0recv)
         spread(l, res)
         if l == 0:
+            zpeers(lambda z2, row: push(aall.at[pl.ds(3, 4), b], aall.at[pl.ds(3, 4), b], AZ + 2, a, row))
             place_terms()
-            done(recv, AZ + 2)
-            forward_a(2, 0, 2)
             form_m0()
             for q in range(2):
                 m0all[q, b] = mbuf[8 * q : 8 * q + 8, :]
         if l == 1:
-            forward_a(2, 2, 2)
+            done(recv, AZ + 2)
+            forward_a(2, 0, 4)
         if l == 2:
             zpeers(lambda z2, row: push(m0all.at[:, b], m0all.at[:, b], MZ, a, row))
         if l == 3:

time: 118 us -> 113 us (0.958)
  Pallas kernels: 115 us -> 110 us
    pallas_call x1, Pallas kernels: 115 us -> 110 us  [shards(): pl.pallas_call(kernel, out_shape=(jax.ShapeDtypeStruct((512, 128), F32),...]
where the time goes in v4:
time: 113 us
  Pallas kernels  110 us (97%)
  local copies, waits for them, and re-layouts  2.28 us (2%)
    pallas_call x1, Pallas kernels, shards(): pl.pallas_call(kernel, out_shape=(jax.ShapeDtypeStruct((512, 128), F32),...  110 us
    unnamed x4, local copies, waits for them, and re-layouts  2.28 us

profile of v4, /device:TPU:1, one launch (start us, length us, event | category | flops | bytes accessed | tf_op | source)
XLA Modules:
  0.0 112.5 jit_solution(13490371689952480757)
XLA Ops:
  0.6 109.6 %shard_map.104 = (f32[512,128]{1,0:T(8,128)}, f32[4,8,128]{2,1,0:T(8,128)}) custom-call(f32[512,128]{1,0:T(8,128)} %bitcast.11, f32[512,512]{1,0:T(8,128)} %bitcast.8, f32[512,512]{1,0:T(8,128)} %bitcast.9, f32[1,512]{1,0:T(1,128)} %bitcast.14, s32[1,4]{1,0:T(1,128)} %bitcast.15, f32[4,8,128]{2,1,0:T(8,128)} %wrhs_in.1, f32[4,8]{1,0:T(4,128)} %wpiv_in.1, ...), custom_call_target="tpu_custom_call" | custom-call | tf_op jit(solution)/shard_map/pallas_call | solution.py:494
  110.2 0.0 copy-start
  110.2 1.7 %copy.13 = f32[1,1,512,128]{3,2,1,0:T(8,128)} copy(f32[1,1,512,128]{3,2,1,0:T(8,128)} %bitcast.10) | data formatting | bytes 524288
  111.9 0.0 copy-done
  111.9 0.6 copy.14
Async XLA Ops:
  110.2 1.7 %copy-start = (f32[4,8,128]{2,1,0:T(8,128)S(1)}, f32[4,8,128]{2,1,0:T(8,128)}, u32[]{:S(2)}) copy-start(f32[4,8,128]{2,1,0:T(8,128)} %get-tuple-element.9) | copy-start | bytes 49156

commit v5 on v4

--- a/solution.py
+++ b/solution.py
@@ -49,8 +49,8 @@
 
 PAT, TERM, USUM, PICK = 0, 1, 2, 3
 AZ, AY, LU, AG, PX, YX, ZX, XX, RS, PY, BX = 4, 7, 10, 14, 18, 22, 26, 30, 34, 38, 42
-U0, X1, MZ, MY, ZA = 46, 47, 48, 49, 50
-NSEM = 51
+U0, X1, MZ, MY, ZA, XS = 46, 47, 48, 49, 50, 51
+NSEM = 52
 
 
 def kernel(rhs_in, inv_in, cpl_in, piv_in, pat_in, wrhs_in, wpiv_in, winv_in, wcpl_in, out_loc, out_win,
@@ -88,7 +88,7 @@
 
     views = {PAT: patrecv.at[pl.ds(0, 7)], TERM: trecv.at[pl.ds(0, 448)], USUM: urecv.at[pl.ds(0, 336)],
              PICK: precv2.at[pl.ds(0, 448)], U0: u0recv.at[pl.ds(0, 248)],
-             X1: x1all.at[:, pl.ds(0, 31)], MZ: m0all.at[:, pl.ds(0, 7)], MY: m0all.at[:, pl.ds(0, 24)],
+             X1: x1all.at[0, pl.ds(0, 31)], XS: x1all.at[0], MZ: m0all.at[:, pl.ds(0, 7)], MY: m0all.at[:, pl.ds(0, 24)],
              ZA: z0all.at[pl.ds(0, 248)]}
     for l in range(LEVELS):
         n = 2**l
@@ -102,8 +102,8 @@
             views[LU + l] = lurecv.at[pl.ds(0, 8 * (n - 1))]
             views[YX + l] = yrecv.at[pl.ds(0, 8 * (n - 1))]
             views[ZX + l] = zbuf.at[pl.ds(0, 8 * (n - 1))]
+        if l > 1:
             views[XX + l] = xbuf.at[pl.ds(0, 8 * (n - 1))]
-        if l > 1:
             views[PY + l] = xpath.at[pl.ds(0, 24 * n)]
     for d in range(1, 4):
         first = 16 if d == 1 else 48
@@ -437,29 +437,32 @@
             picked = mm(chosen, pieces[0]) + mm(chosen, pieces[1])
             for j in range(16):
                 psend[pl.ds(j, 32, stride=16), :] = picked[:, 128 * j : 128 * j + 128]
-            zpeers(lambda z2, row: push(psend.at[pl.ds(at8(z2 * 64), 64)], precv2.at[pl.ds(own64, 64)], PICK, a, row))
             precv2[pl.ds(own64, 64), :] = psend[pl.ds(own64, 64), :]
         value = reduced(l, zs[l])
-        at = at8(TOP[l] + lax.rem(a, n) * 8)
-        xbuf[pl.ds(at, 8), :] = value
-        mine = xbuf.at[pl.ds(at, 8)]
-        for d in range(1, n):
-            push(mine, mine, XX + l, flip(a, d), b)
-        out_win[l] = value
-        done(recv, XX + l)
-        level = xbuf[TOP[l] : TOP[l] + 8 * n, :]
         if l > 1:
+            at = at8(TOP[l] + lax.rem(a, n) * 8)
+            xbuf[pl.ds(at, 8), :] = value
+            mine = xbuf.at[pl.ds(at, 8)]
+            for d in range(1, n):
+                push(mine, mine, XX + l, flip(a, d), b)
+            out_win[l] = value
+            done(recv, XX + l)
+            level = xbuf[TOP[l] : TOP[l] + 8 * n, :]
             reduce_rows(l - 1, ahead - dot3(m_t, fill(level, LINK[l - 1])), None)
             block = xbuf.at[pl.ds(TOP[l], 8 * n)]
             there = xpath.at[pl.ds(at8(y * 128 + TOP[l]), 8 * n)]
             ypeers(lambda row: push(block, there, PY + l, a, row))
             xpath[pl.ds(at8(y * 128 + TOP[l]), 8 * n), :] = level
         else:
-            for q in range(2):
-                x1all[q, b] = level[8 * q : 8 * q + 8]
-            rowpeers(lambda row: push(x1all.at[:, b], x1all.at[:, b], X1, a, row))
+            half = lax.rem(a, 2)
+            x1all[half, b] = value
+            rowpeers(lambda row: push(x1all.at[half, b], x1all.at[half, b], X1, a, row))
+            zpeers(lambda z2, row: push(psend.at[pl.ds(at8(z2 * 64), 64)], precv2.at[pl.ds(own64, 64)], PICK, a, row))
+            out_win[l] = value
 
     done(recv, X1)
+    push(x1all.at[half], x1all.at[half], XS, flip(a, 1), b)
+    done(recv, XS)
     x1 = x1all[...].reshape(512, 128)
     x0all[...] = c0[...] - dot3((m0t_h[...], m0t_l[...]), split(x1))
     out_win[0] = x0all[pl.ds(own8, 8), :]

time: 113 us -> 111 us (0.982)
  Pallas kernels: 110 us -> 108 us
    pallas_call x1, Pallas kernels: 110 us -> 108 us  [shards(): pl.pallas_call(kernel, out_shape=(jax.ShapeDtypeStruct((512, 128), F32),...]
where the time goes in v5:
time: 111 us
  Pallas kernels  108 us (97%)
  local copies, waits for them, and re-layouts  2.28 us (2%)
    pallas_call x1, Pallas kernels, shards(): pl.pallas_call(kernel, out_shape=(jax.ShapeDtypeStruct((512, 128), F32),...  108 us
    unnamed x4, local copies, waits for them, and re-layouts  2.28 us

profile of v5, /device:TPU:1, one launch (start us, length us, event | category | flops | bytes accessed | tf_op | source)
XLA Modules:
  0.0 110.7 jit_solution(9354948153229568021)
XLA Ops:
  0.6 107.7 %shard_map.104 = (f32[512,128]{1,0:T(8,128)}, f32[4,8,128]{2,1,0:T(8,128)}) custom-call(f32[512,128]{1,0:T(8,128)} %bitcast.11, f32[512,512]{1,0:T(8,128)} %bitcast.8, f32[512,512]{1,0:T(8,128)} %bitcast.9, f32[1,512]{1,0:T(1,128)} %bitcast.14, s32[1,4]{1,0:T(1,128)} %bitcast.15, f32[4,8,128]{2,1,0:T(8,128)} %wrhs_in.1, f32[4,8]{1,0:T(4,128)} %wpiv_in.1, ...), custom_call_target="tpu_custom_call" | custom-call | tf_op jit(solution)/shard_map/pallas_call | solution.py:497
  108.4 0.0 copy-start
  108.4 1.7 %copy.13 = f32[1,1,512,128]{3,2,1,0:T(8,128)} copy(f32[1,1,512,128]{3,2,1,0:T(8,128)} %bitcast.10) | data formatting | bytes 524288
  110.1 0.0 copy-done
  110.1 0.6 copy.14
Async XLA Ops:
  108.4 1.7 %copy-start = (f32[4,8,128]{2,1,0:T(8,128)S(1)}, f32[4,8,128]{2,1,0:T(8,128)}, u32[]{:S(2)}) copy-start(f32[4,8,128]{2,1,0:T(8,128)} %get-tuple-element.9) | copy-start | bytes 49156

commit v6 on v5

--- a/solution.py
+++ b/solution.py
@@ -130,14 +130,18 @@
 
         lax.fori_loop(0, NY - 1, step, 0)
 
+    ring_y = [lax.rem(y + d, NY) * NZ for d in (2, 1, 3, 0)]
+
     def rowpeers(body):
         def step(k, carry):
-            y2 = lax.rem(y + around(lax.rem(k, NY), NY), NY)
-            z2 = lax.rem(z + around(lax.div(k, NY), NZ), NZ)
-            body(y2 * NZ + z2)
+            z2 = lax.rem(z + around(k, NZ), NZ)
+            for y2 in ring_y:
+                body(y2 + z2)
             return carry
 
-        lax.fori_loop(0, NB - 1, step, 0)
+        lax.fori_loop(0, NZ - 1, step, 0)
+        for y2 in ring_y[:-1]:
+            body(y2 + z)
 
     sel[...] = jnp.zeros((128, 128), F32)
     xpath[...] = jnp.zeros((512, 128), F32)
@@ -356,6 +360,9 @@
             forward_a(2, 0, 4)
         if l == 2:
             zpeers(lambda z2, row: push(m0all.at[:, b], m0all.at[:, b], MZ, a, row))
+        if l == 2:
+            z0all[pl.ds(own8, 8), :] = zs[0]
+            rowpeers(lambda row: push(z0all.at[pl.ds(own8, 8)], z0all.at[pl.ds(own8, 8)], ZA, a, row))
         if l == 3:
             done(recv, MZ)
             slab0 = m0all.at[:, pl.ds(y * NZ, NZ)]
@@ -382,8 +389,6 @@
             below = collect(PX + l, precv, SLOT[l + 1], 2 * n, below)
         pending = (res, own_y)
     zs.append(keep_z(3, *pending))
-    z0all[pl.ds(own8, 8), :] = zs[0]
-    rowpeers(lambda row: push(z0all.at[pl.ds(own8, 8)], z0all.at[pl.ds(own8, 8)], ZA, a, row))
 
     def fill(value, first):
         before = [jnp.zeros((first, 128), F32)] if first else []

time: 111 us -> 110 us (level)
  no operation moved by 1% of the time
where the time goes in v6:
time: 110 us
  Pallas kernels  107 us (97%)
  local copies, waits for them, and re-layouts  2.28 us (2%)
    pallas_call x1, Pallas kernels, shards(): pl.pallas_call(kernel, out_shape=(jax.ShapeDtypeStruct((512, 128), F32),...  107 us
    unnamed x4, local copies, waits for them, and re-layouts  2.28 us

profile of v6, /device:TPU:1, one launch (start us, length us, event | category | flops | bytes accessed | tf_op | source)
XLA Modules:
  0.0 109.6 jit_solution(1473443428618069191)
XLA Ops:
  0.6 106.6 %shard_map.104 = (f32[512,128]{1,0:T(8,128)}, f32[4,8,128]{2,1,0:T(8,128)}) custom-call(f32[512,128]{1,0:T(8,128)} %bitcast.11, f32[512,512]{1,0:T(8,128)} %bitcast.8, f32[512,512]{1,0:T(8,128)} %bitcast.9, f32[1,512]{1,0:T(1,128)} %bitcast.14, s32[1,4]{1,0:T(1,128)} %bitcast.15, f32[4,8,128]{2,1,0:T(8,128)} %wrhs_in.1, f32[4,8]{1,0:T(4,128)} %wpiv_in.1, ...), custom_call_target="tpu_custom_call" | custom-call | tf_op jit(solution)/shard_map/pallas_call | solution.py:502
  107.3 0.0 copy-start
  107.3 1.7 %copy.13 = f32[1,1,512,128]{3,2,1,0:T(8,128)} copy(f32[1,1,512,128]{3,2,1,0:T(8,128)} %bitcast.10) | data formatting | bytes 524288
  109.0 0.0 copy-done
  109.0 0.6 copy.14
Async XLA Ops:
  107.3 1.7 %copy-start = (f32[4,8,128]{2,1,0:T(8,128)S(1)}, f32[4,8,128]{2,1,0:T(8,128)}, u32[]{:S(2)}) copy-start(f32[4,8,128]{2,1,0:T(8,128)} %get-tuple-element.9) | copy-start | bytes 49156
